TPU v7x, 128 devices: a whole 4x4x4 slice. The times are simulated.
128 devices in a mesh: lat: 16 (over y_lo, z, core), lon: 4 (over x), rep: 2 (over y_hi).
Axes of the slice: x: 4, y: 4 (y_hi: 2, y_lo: 2; y = y_hi * 2 + y_lo), z: 4, core: 2. Of those that a mesh axis runs over, the one named last changes fastest.
Arguments:
- latent: bfloat16 [6, 96, 384, 512], P('rep', 'lat', 'lon'), parts along dimension 0, may hold values from -6 to 6
- band_labels: int32 [96], replicated, may hold values from 0 to 23, never falling along the last dimension, each value on 1 to 8 neighbouring positions
- gain_first: float32 [512], replicated, may hold values from 0.1 to 1.9
- qkv_first: bfloat16 [512, 1536], replicated, may hold values from -2 to 2
- proj_first: bfloat16 [512, 512], replicated, may hold values from -1 to 1
- merge_gain: float32 [2048], replicated, may hold values from 0.1 to 1.9
- merge_weight: bfloat16 [2048, 1024], replicated, may hold values from -0.125 to 0.125
- gain_coarse: float32 [1024], replicated, may hold values from 0.1 to 1.9
- qkv_coarse: bfloat16 [1024, 3072], replicated, may hold values from -2 to 2
- proj_coarse: bfloat16 [1024, 1024], replicated, may hold values from -0.75 to 0.75
- split_gain: float32 [1024], replicated, may hold values from 0.1 to 1.9
- split_weight: bfloat16 [1024, 2048], replicated, may hold values from -0.1875 to 0.1875
- gain_last: float32 [512], replicated, may hold values from 0.1 to 1.9
- qkv_last: bfloat16 [512, 1536], replicated, may hold values from -2 to 2
- proj_last: bfloat16 [512, 512], replicated, may hold values from -1 to 1
Outputs:
- forecast_latent: bfloat16 [6, 96, 384, 512], P('rep', 'lat', 'lon'), parts along dimension 0
There are 2 independent parts, one for each index of `rep`. A program takes and returns all parts, laid end to end along the dimension named above; an argument that names none is the same for every part. Nothing has to cross between parts.
Inputs may be any that keep to these rules, and one draw needn't show every extreme that they name: `band_labels`: labels never fall along the rows, and each label covers 1 to 8 consecutive rows.
All inputs are finite; a program needn't handle non-finite values.
Results may differ from a plain program's by a relative error of at most 0.015.
Values may be sent and summed in bfloat16 or wider, within the bound.
A program may use at most 128 MiB of HBM per device.

v0:
```python
import jax
import jax.numpy as jnp
from jax import lax
from jax.experimental import pallas as pl
from jax.experimental.pallas import tpu as pltpu
from jax.sharding import PartitionSpec as P

NT = (((1,), (1,)), ((), ()))
TN = (((0,), (0,)), ((), ()))
f32 = jnp.float32
bf16 = jnp.bfloat16


def norm(x, g):
    c = jnp.mean(x, axis=-1, keepdims=True)
    d = x - c
    s = jnp.mean(d * d, axis=-1, keepdims=True)
    return (d * lax.rsqrt(s + 1e-05) * g).astype(bf16)


def attend_window(x, g, wqkv_ref, wvt_ref, wo_ref, qk_s, vt_s, ot_s, bias_ref):
    E = x.shape[1]
    h = norm(x, g)
    q = jnp.dot(h, wqkv_ref[:, :E], preferred_element_type=f32)
    qk_s[:, :E] = q.astype(bf16) * bf16(0.125)
    k = jnp.dot(h, wqkv_ref[:, E : 2 * E], preferred_element_type=f32)
    qk_s[:, E : 2 * E] = k.astype(bf16)
    vt = lax.dot_general(wvt_ref[...], h, NT, preferred_element_type=f32)
    vt_s[...] = vt.astype(bf16)
    lane = lax.broadcasted_iota(jnp.int32, (216, 128), 1)
    for hp in range(E // 128):
        qb = qk_s[:, 128 * hp : 128 * hp + 128]
        kb = qk_s[:, E + 128 * hp : E + 128 * hp + 128]
        for half in range(2):
            qm = jnp.where((lane >= 64) if half else (lane < 64), qb, bf16(0))
            st = lax.dot_general(kb, qm, NT, preferred_element_type=f32)
            if bias_ref is not None:
                st = st + bias_ref[...]
            m = jnp.max(st, axis=0, keepdims=True)
            e = jnp.exp(st - m)
            d = jnp.sum(e, axis=0, keepdims=True)
            hd = 64 * (2 * hp + half)
            ot = jnp.dot(vt_s[hd : hd + 64, :], e.astype(bf16), preferred_element_type=f32)
            ot_s[hd : hd + 64, :] = (ot * (1.0 / d)).astype(bf16)
    y = lax.dot_general(ot_s[...], wo_ref[...], TN, preferred_element_type=f32)
    return x + y


def token_label(t, lab_ref, start):
    t = t - jnp.where(t >= 144, 144, jnp.where(t >= 72, 72, 0))
    n = lab_ref.shape[0]
    out = jnp.zeros(t.shape, jnp.int32)
    for r in range(6):
        lab = lab_ref[lax.rem(start + r + n, n)]
        out = jnp.where(t >= 12 * r, lab, out)
    return out


def fill_bias(bias_ref, lab_ref, start):
    kt = token_label(lax.broadcasted_iota(jnp.int32, (216, 216), 0), lab_ref, start)
    qt = token_label(lax.broadcasted_iota(jnp.int32, (216, 216), 1), lab_ref, start)
    bias_ref[...] = jnp.where(kt == qt, f32(0), f32(-1e30))


def fine_kernel(lab_ref, x_ref, g_ref, wqkv_ref, wo_ref, o_ref, xw, wvt, bias, qk_s, vt_s, ot_s):
    fill_bias(bias, lab_ref, lax.axis_index("lat") * 6 + 3)
    wvt[...] = wqkv_ref[:, 1024:1536].T
    for lr in range(18):
        slab = x_ref[lr // 6, lr % 6].astype(f32)
        for w in range(8):
            xw[w, 12 * lr : 12 * lr + 12, :] = slab[12 * w : 12 * w + 12]

    def window(w, carry):
        xw[w] = attend_window(xw[w], g_ref[...], wqkv_ref, wvt, wo_ref, qk_s, vt_s, ot_s, bias)
        return carry

    lax.fori_loop(0, 8, window, 0)
    for lr in range(18):
        slab = jnp.concatenate([xw[w, 12 * lr : 12 * lr + 12, :] for w in range(8)], axis=0)
        o_ref[lr // 6, lr % 6] = slab.astype(bf16)


def fine_call(labels, x, g, wqkv, wo):
    V = pl.BlockSpec(memory_space=pltpu.VMEM)
    return pl.pallas_call(
        fine_kernel,
        out_shape=jax.ShapeDtypeStruct(x.shape, bf16),
        in_specs=[pl.BlockSpec(memory_space=pltpu.SMEM), V, V, V, V],
        out_specs=V,
        scratch_shapes=[
            pltpu.VMEM((8, 216, 512), f32),
            pltpu.VMEM((512, 512), bf16),
            pltpu.VMEM((216, 216), f32),
            pltpu.VMEM((216, 1024), bf16),
            pltpu.VMEM((512, 216), bf16),
            pltpu.VMEM((512, 216), bf16),
        ],
        compiler_params=pltpu.CompilerParams(vmem_limit_bytes=60 << 20),
        cost_estimate=pl.CostEstimate(flops=5 * 10**9, bytes_accessed=6 * 10**6, transcendentals=3 * 10**6),
        name="fine",
    )(labels, x, g.reshape(1, -1), wqkv, wo)


def vm():
    return pl.BlockSpec(memory_space=pltpu.VMEM)


def merge_kernel(x_ref, g_ref, w_ref, o_ref, tmp, h_s):
    for i in range(9):
        l, rr = i // 3, i % 3
        for r in range(2):
            for j in range(4):
                tmp[r, j] = x_ref[l, 2 * rr + r, :, 128 * j : 128 * j + 128].astype(f32)
        parts = [tmp[r, j, pl.ds(c, 48, stride=2), :] for c in range(2) for r in range(2) for j in range(4)]
        h_s[48 * i : 48 * i + 48, :] = norm(jnp.concatenate(parts, axis=1), g_ref[...])
    for n in range(4):
        y = jnp.dot(h_s[...], w_ref[:, 256 * n : 256 * n + 256], preferred_element_type=f32).astype(bf16)
        for i in range(9):
            o_ref[i // 3, i % 3, :, 256 * n : 256 * n + 256] = y[48 * i : 48 * i + 48]


def merge_call(x, g, w):
    return pl.pallas_call(
        merge_kernel,
        out_shape=jax.ShapeDtypeStruct((3, 3, 48, 1024), bf16),
        in_specs=[vm()] * 3,
        out_specs=vm(),
        scratch_shapes=[pltpu.VMEM((2, 4, 96, 128), f32), pltpu.VMEM((432, 2048), bf16)],
        compiler_params=pltpu.CompilerParams(vmem_limit_bytes=60 << 20),
        cost_estimate=pl.CostEstimate(flops=2 * 10**9, bytes_accessed=7 * 10**6, transcendentals=10**3),
        name="merge",
    )(x, g.reshape(1, -1), w)


def coarse_kernel(x_ref, g_ref, wqkv_ref, wo_ref, o_ref, xw, wvt, qk_s, vt_s, ot_s):
    wvt[...] = wqkv_ref[:, 2048:3072].T
    for lr in range(18):
        slab = x_ref[lr // 6, lr % 6].astype(f32)
        for w in range(2):
            xw[w, 12 * lr : 12 * lr + 12, :] = slab[12 * w : 12 * w + 12]

    def window(w, carry):
        xw[w] = attend_window(xw[w], g_ref[...], wqkv_ref, wvt, wo_ref, qk_s, vt_s, ot_s, None)
        return carry

    lax.fori_loop(0, 2, window, 0)
    for lr in range(18):
        slab = jnp.concatenate([xw[w, 12 * lr : 12 * lr + 12, :] for w in range(2)], axis=0)
        o_ref[lr // 6, lr % 6] = slab.astype(bf16)


def coarse_call(x, g, wqkv, wo):
    return pl.pallas_call(
        coarse_kernel,
        out_shape=jax.ShapeDtypeStruct(x.shape, bf16),
        in_specs=[vm()] * 4,
        out_specs=vm(),
        scratch_shapes=[
            pltpu.VMEM((2, 216, 1024), f32),
            pltpu.VMEM((1024, 1024), bf16),
            pltpu.VMEM((216, 2048), bf16),
            pltpu.VMEM((1024, 216), bf16),
            pltpu.VMEM((1024, 216), bf16),
        ],
        compiler_params=pltpu.CompilerParams(vmem_limit_bytes=60 << 20),
        cost_estimate=pl.CostEstimate(flops=5 * 10**9, bytes_accessed=11 * 10**6, transcendentals=2 * 10**6),
        name="coarse",
    )(x, g.reshape(1, -1), wqkv, wo)


def split_kernel(c_ref, x_ref, g_ref, w_ref, o_ref, tmp, h_s, sp_s):
    for i in range(9):
        h_s[48 * i : 48 * i + 48, :] = norm(c_ref[i // 3, i % 3].astype(f32), g_ref[...])
    for n in range(8):
        sp_s[:, 256 * n : 256 * n + 256] = jnp.dot(
            h_s[...], w_ref[:, 256 * n : 256 * n + 256], preferred_element_type=f32
        )
    for i in range(9):
        l, rr = i // 3, i % 3
        for p in range(4):
            for j in range(4):
                c = 512 * p + 128 * j
                tmp[p % 2, j, pl.ds(p // 2, 48, stride=2), :] = sp_s[48 * i : 48 * i + 48, c : c + 128]
        for r in range(2):
            for j in range(4):
                c = slice(128 * j, 128 * j + 128)
                o_ref[l, 2 * rr + r, :, c] = (x_ref[l, 2 * rr + r, :, c].astype(f32) + tmp[r, j]).astype(bf16)


def split_call(c, x, g, w):
    return pl.pallas_call(
        split_kernel,
        out_shape=jax.ShapeDtypeStruct(x.shape, bf16),
        in_specs=[vm()] * 4,
        out_specs=vm(),
        scratch_shapes=[
            pltpu.VMEM((2, 4, 96, 128), f32),
            pltpu.VMEM((432, 1024), bf16),
            pltpu.VMEM((432, 2048), f32),
        ],
        compiler_params=pltpu.CompilerParams(vmem_limit_bytes=60 << 20),
        cost_estimate=pl.CostEstimate(flops=2 * 10**9, bytes_accessed=8 * 10**6, transcendentals=10**3),
        name="split",
    )(c, x, g.reshape(1, -1), w)


def shift(value, axis, steps):
    count = lax.axis_size(axis)
    return lax.ppermute(value, axis, [(s, (s + steps) % count) for s in range(count)])


def swap_band(value):
    count = lax.axis_size("lat")
    pairs = [(s, (s + (1 if s % 2 else -1)) % count) for s in range(count)]
    return lax.ppermute(value, "lat", pairs)


def roll_ahead(field):
    wide = jnp.concatenate([field[:, :, 6:], shift(field[:, :, :6], "lon", -1)], axis=2)
    return jnp.concatenate([wide[:, 3:], shift(wide[:, :3], "lat", -1)], axis=1)


def roll_behind(field):
    tall = jnp.concatenate([shift(field[:, -3:], "lat", 1), field[:, :-3]], axis=1)
    return jnp.concatenate([shift(tall[:, :, -6:], "lon", 1), tall[:, :, :-6]], axis=2)


def fine_block(field, gain, qkv, proj, labels):
    return roll_behind(fine_call(labels, roll_ahead(field), gain, qkv, proj))


def coarse_block(merged, gain, qkv, proj):
    odd = lax.axis_index("lat") % 2
    wide = jnp.concatenate([merged[:, :, 6:], shift(merged[:, :, :6], "lon", -1)], axis=2)
    mine = lax.dynamic_slice_in_dim(wide, 24 * (1 - odd), 24, 2)
    other = swap_band(lax.dynamic_slice_in_dim(wide, 24 * odd, 24, 2))
    done = coarse_call(jnp.concatenate([mine, other], axis=1), gain, qkv, proj)
    back = swap_band(done[:, 3:])
    kept = done[:, :3]
    left = jnp.where(odd == 1, kept, back)
    right = jnp.where(odd == 1, back, kept)
    return jnp.concatenate([shift(right[:, :, 18:], "lon", 1), left, right[:, :, :18]], axis=2)


def body(
    latent,
    band_labels,
    gain_first,
    qkv_first,
    proj_first,
    merge_gain,
    merge_weight,
    gain_coarse,
    qkv_coarse,
    proj_coarse,
    split_gain,
    split_weight,
    gain_last,
    qkv_last,
    proj_last,
):
    first = fine_block(latent, gain_first, qkv_first, proj_first, band_labels)
    merged = merge_call(first, merge_gain, merge_weight)
    coarse = coarse_block(merged, gain_coarse, qkv_coarse, proj_coarse)
    joined = split_call(coarse, first, split_gain, split_weight)
    return fine_block(joined, gain_last, qkv_last, proj_last, band_labels)


def solution(mesh):
    return jax.shard_map(
        body,
        mesh=mesh,
        in_specs=(P("rep", "lat", "lon", None),) + (P(),) * 14,
        out_specs=P("rep", "lat", "lon", None),
        check_vma=False,
    )
```

profile of v0, /device:TPU:0, one launch (start us, length us, event | category | flops | bytes accessed | tf_op | source)
XLA Modules:
  0.0 211.7 jit_solution(6464356982582670886)
XLA Ops:
  0.9 2.9 %collective-permute-start = (bf16[3,6,6,512]{3,2,1,0:T(8,128)(2,1)S(1)}, bf16[3,6,6,512]{3,2,1,0:T(8,128)(2,1)S(1)}, u32[]{:S(2)}, u32[]{:S(2)}) collective-permute-start(bf16[3,6,6,512]{3,2,1,0:T(8,128)(2,1)S(1)} %slice.67), channel_id=1, source_target_pairs={{0,6},{2,0},{4,2},{6,4},{1,7},{3,1},{5,3},{7,5},{8,14},{10,8},{12,... | collective-permute-start | bytes 331784 | tf_op jit(solution)/shard_map/ppermute | solution.py:209
  3.9 2.3 %slice.66 = bf16[3,6,90,512]{3,2,1,0:T(8,128)(2,1)S(1)} slice(bf16[3,6,96,512]{3,2,1,0:T(8,128)(2,1)} %param.15), slice={[0:3], [0:6], [6:96], [0:512]} | slice | bytes 3317760 | tf_op jit(solution)/shard_map/slice | solution.py:219
  7.1 3.7 %collective-permute-start.1 = (bf16[3,3,96,512]{3,2,1,0:T(8,128)(2,1)S(1)}, bf16[3,3,96,512]{3,2,1,0:T(8,128)(2,1)S(1)}, u32[]{:S(2)}, u32[]{:S(2)}) collective-permute-start(bf16[3,3,96,512]{3,2,1,0:T(8,128)(2,1)S(1)} %get-tuple-element.8), channel_id=1, source_target_pairs={{0,120},{8,0},{16,8},{24,16},{32,24},{40,32},{48,40},{56,48},{64,5... | collective-permute-start | bytes 2654216 | tf_op jit(solution)/shard_map/ppermute | solution.py:209
  10.8 10.6 %collective-permute-done.1 = bf16[3,3,96,512]{3,2,1,0:T(8,128)(2,1)S(1)} collective-permute-done((bf16[3,3,96,512]{3,2,1,0:T(8,128)(2,1)S(1)}, bf16[3,3,96,512]{3,2,1,0:T(8,128)(2,1)S(1)}, u32[]{:S(2)}, u32[]{:S(2)}) %collective-permute-start.1) | collective-permute-done | bytes 884768 | tf_op jit(solution)/shard_map/ppermute | solution.py:209
  21.4 1.4 pad_maximum_fusion.2.x_ref
  22.8 25.0 %fine.2 = bf16[3,6,96,512]{3,2,1,0:T(8,128)(2,1)} custom-call(s32[96]{0:T(128)} %lab_ref.3, bf16[3,6,96,512]{3,2,1,0:T(8,128)(2,1)} %pad_maximum_fusion.2.x_ref, f32[1,512]{1,0:T(1,128)} %bitcast.10, bf16[512,1536]{1,0:T(8,128)(2,1)} %wqkv_ref.3, bf16[512,512]{1,0:T(8,128)(2,1)} %wo_ref.3), custom_call_target="tpu_custom_call" | custom-call | flops 5000000000 | bytes 6000000 | tf_op jit(solution)/shard_map/fine/pallas_call | solution.py:85
  47.8 1.5 fusion.7
  49.4 14.7 %collective-permute-done.2 = bf16[3,3,96,512]{3,2,1,0:T(8,128)(2,1)S(1)} collective-permute-done((bf16[3,3,96,512]{3,2,1,0:T(8,128)(2,1)S(1)}, bf16[3,3,96,512]{3,2,1,0:T(8,128)(2,1)S(1)}, u32[]{:S(2)}, u32[]{:S(2)}) %collective-permute-start.2) | collective-permute-done | bytes 884768 | tf_op jit(solution)/shard_map/ppermute | solution.py:209
  64.2 1.3 collective-permute-start.3
  65.5 5.6 %collective-permute-done.3 = bf16[3,6,6,512]{3,2,1,0:T(8,128)(2,1)S(1)} collective-permute-done((bf16[3,6,6,512]{3,2,1,0:T(8,128)(2,1)S(1)}, bf16[3,6,6,512]{3,2,1,0:T(8,128)(2,1)S(1)}, u32[]{:S(2)}, u32[]{:S(2)}) %collective-permute-start.3) | collective-permute-done | bytes 110624 | tf_op jit(solution)/shard_map/ppermute | solution.py:209
  71.1 2.0 fusion.1.x_ref
  73.1 6.6 %merge.1 = bf16[3,3,48,1024]{3,2,1,0:T(8,128)(2,1)} custom-call(bf16[3,6,96,512]{3,2,1,0:T(8,128)(2,1)} %fusion.1.x_ref, f32[1,2048]{1,0:T(1,128)} %bitcast.8, bf16[2048,1024]{1,0:T(8,128)(2,1)} %w_ref.2), custom_call_target="tpu_custom_call" | custom-call | flops 2000000000 | bytes 7000000 | tf_op jit(solution)/shard_map/merge/pallas_call | solution.py:123
  80.7 2.1 collective-permute-start.4
  82.8 1.4 slice.92
  84.1 1.7 collective-permute-done.4
  86.9 9.8 %collective-permute-done.5 = bf16[3,3,24,1024]{3,2,1,0:T(8,128)(2,1)S(1)} collective-permute-done((bf16[3,3,24,1024]{3,2,1,0:T(8,128)(2,1)S(1)}, bf16[3,3,24,1024]{3,2,1,0:T(8,128)(2,1)S(1)}, u32[]{:S(2)}, u32[]{:S(2)}) %collective-permute-start.5) | collective-permute-done | bytes 442400 | tf_op jit(solution)/shard_map/ppermute | solution.py:215
  97.7 18.9 %coarse.1 = bf16[3,6,24,1024]{3,2,1,0:T(8,128)(2,1)} custom-call(bf16[3,6,24,1024]{3,2,1,0:T(8,128)(2,1)} %pad_maximum_fusion.6.x_ref, f32[1,1024]{1,0:T(1,128)} %bitcast.9, bf16[1024,3072]{1,0:T(8,128)(2,1)} %wqkv_ref.4, bf16[1024,1024]{1,0:T(8,128)(2,1)} %wo_ref.4), custom_call_target="tpu_custom_call" | custom-call | flops 5000000000 | bytes 11000000 | tf_op jit(solution)/shard_map/coarse/pallas_call | solution.py:153
  116.6 1.0 slice.94
  117.7 9.8 %collective-permute-done.6 = bf16[3,3,24,1024]{3,2,1,0:T(8,128)(2,1)S(1)} collective-permute-done((bf16[3,3,24,1024]{3,2,1,0:T(8,128)(2,1)S(1)}, bf16[3,3,24,1024]{3,2,1,0:T(8,128)(2,1)S(1)}, u32[]{:S(2)}, u32[]{:S(2)}) %collective-permute-start.6) | collective-permute-done | bytes 442400 | tf_op jit(solution)/shard_map/ppermute | solution.py:215
  127.6 1.1 broadcast_select_fusion
  128.8 6.3 %collective-permute-done.7 = bf16[3,3,6,1024]{3,2,1,0:T(8,128)(2,1)S(1)} collective-permute-done((bf16[3,3,6,1024]{3,2,1,0:T(8,128)(2,1)S(1)}, bf16[3,3,6,1024]{3,2,1,0:T(8,128)(2,1)S(1)}, u32[]{:S(2)}, u32[]{:S(2)}) %collective-permute-start.7) | collective-permute-done | bytes 110624 | tf_op jit(solution)/shard_map/ppermute | solution.py:209
  135.1 1.2 pad_maximum_fusion.7.c_ref
  136.3 6.9 %split.1 = bf16[3,6,96,512]{3,2,1,0:T(8,128)(2,1)} custom-call(bf16[3,3,48,1024]{3,2,1,0:T(8,128)(2,1)} %pad_maximum_fusion.7.c_ref, bf16[3,6,96,512]{3,2,1,0:T(8,128)(2,1)} %fusion.1.x_ref, f32[1,1024]{1,0:T(1,128)} %bitcast.7, bf16[1024,2048]{1,0:T(8,128)(2,1)} %w_ref.3), custom_call_target="tpu_custom_call" | custom-call | flops 2000000000 | bytes 8000000 | tf_op jit(solution)/shard_map/split/pallas_call | solution.py:191
  144.2 2.1 collective-permute-start.8
  146.3 2.3 %slice.98 = bf16[3,6,90,512]{3,2,1,0:T(8,128)(2,1)S(1)} slice(bf16[3,6,96,512]{3,2,1,0:T(8,128)(2,1)} %split.1), slice={[0:3], [0:6], [6:96], [0:512]} | slice | bytes 3317760 | tf_op jit(solution)/shard_map/slice | solution.py:219
  149.9 10.6 %collective-permute-done.9 = bf16[3,3,96,512]{3,2,1,0:T(8,128)(2,1)S(1)} collective-permute-done((bf16[3,3,96,512]{3,2,1,0:T(8,128)(2,1)S(1)}, bf16[3,3,96,512]{3,2,1,0:T(8,128)(2,1)S(1)}, u32[]{:S(2)}, u32[]{:S(2)}) %collective-permute-start.9) | collective-permute-done | bytes 884768 | tf_op jit(solution)/shard_map/ppermute | solution.py:209
  160.4 1.4 pad_maximum_fusion.3.x_ref
  161.8 25.0 %fine.3 = bf16[3,6,96,512]{3,2,1,0:T(8,128)(2,1)} custom-call(s32[96]{0:T(128)} %lab_ref.3, bf16[3,6,96,512]{3,2,1,0:T(8,128)(2,1)} %pad_maximum_fusion.3.x_ref, f32[1,512]{1,0:T(1,128)} %bitcast.11, bf16[512,1536]{1,0:T(8,128)(2,1)} %wqkv_ref.5, bf16[512,512]{1,0:T(8,128)(2,1)} %wo_ref.5), custom_call_target="tpu_custom_call" | custom-call | flops 5000000000 | bytes 6000000 | tf_op jit(solution)/shard_map/fine/pallas_call | solution.py:85
  186.8 1.5 fusion.6
  188.5 14.7 %collective-permute-done.10 = bf16[3,3,96,512]{3,2,1,0:T(8,128)(2,1)S(1)} collective-permute-done((bf16[3,3,96,512]{3,2,1,0:T(8,128)(2,1)S(1)}, bf16[3,3,96,512]{3,2,1,0:T(8,128)(2,1)S(1)}, u32[]{:S(2)}, u32[]{:S(2)}) %collective-permute-start.10) | collective-permute-done | bytes 884768 | tf_op jit(solution)/shard_map/ppermute | solution.py:209
  203.3 6.3 %collective-permute-done.11 = bf16[3,6,6,512]{3,2,1,0:T(8,128)(2,1)S(1)} collective-permute-done((bf16[3,6,6,512]{3,2,1,0:T(8,128)(2,1)S(1)}, bf16[3,6,6,512]{3,2,1,0:T(8,128)(2,1)S(1)}, u32[]{:S(2)}, u32[]{:S(2)}) %collective-permute-start.11) | collective-permute-done | bytes 110624 | tf_op jit(solution)/shard_map/ppermute | solution.py:209
  209.7 2.0 fusion
  (19 shorter events, 7.5 us)
Async XLA Ops:
  0.9 6.0 %collective-permute-start = (bf16[3,6,6,512]{3,2,1,0:T(8,128)(2,1)S(1)}, bf16[3,6,6,512]{3,2,1,0:T(8,128)(2,1)S(1)}, u32[]{:S(2)}, u32[]{:S(2)}) collective-permute-start(bf16[3,6,6,512]{3,2,1,0:T(8,128)(2,1)S(1)} %slice.67), channel_id=1, source_target_pairs={{0,6},{2,0},{4,2},{6,4},{1,7},{3,1},{5,3},{7,5},{8,14},{10,8},{12,... | collective-permute-start | bytes 331784 | tf_op jit(solution)/shard_map/ppermute | solution.py:209
  7.1 14.3 %collective-permute-start.1 = (bf16[3,3,96,512]{3,2,1,0:T(8,128)(2,1)S(1)}, bf16[3,3,96,512]{3,2,1,0:T(8,128)(2,1)S(1)}, u32[]{:S(2)}, u32[]{:S(2)}) collective-permute-start(bf16[3,3,96,512]{3,2,1,0:T(8,128)(2,1)S(1)} %get-tuple-element.8), channel_id=1, source_target_pairs={{0,120},{8,0},{16,8},{24,16},{32,24},{40,32},{48,40},{56,48},{64,5... | collective-permute-start | bytes 2654216 | tf_op jit(solution)/shard_map/ppermute | solution.py:209
  49.3 14.8 %collective-permute-start.2 = (bf16[3,3,96,512]{3,2,1,0:T(8,128)(2,1)S(1)}, bf16[3,3,96,512]{3,2,1,0:T(8,128)(2,1)S(1)}, u32[]{:S(2)}, u32[]{:S(2)}) collective-permute-start(bf16[3,3,96,512]{3,2,1,0:T(8,128)(2,1)S(1)} %get-tuple-element.11), channel_id=1, source_target_pairs={{0,8},{8,16},{16,24},{24,32},{32,40},{40,48},{48,56},{56,64},{64,7... | collective-permute-start | bytes 2654216 | tf_op jit(solution)/shard_map/ppermute | solution.py:209
  64.2 6.9 %collective-permute-start.3 = (bf16[3,6,6,512]{3,2,1,0:T(8,128)(2,1)S(1)}, bf16[3,6,6,512]{3,2,1,0:T(8,128)(2,1)S(1)}, u32[]{:S(2)}, u32[]{:S(2)}) collective-permute-start(bf16[3,6,6,512]{3,2,1,0:T(8,128)(2,1)S(1)} %pad_maximum_fusion.9), channel_id=1, source_target_pairs={{0,2},{2,4},{4,6},{6,0},{1,3},{3,5},{5,7},{7,1},{8,10},{10,12},{12... | collective-permute-start | bytes 331784 | tf_op jit(solution)/shard_map/ppermute | solution.py:209
  80.7 5.2 %collective-permute-start.4 = (bf16[3,3,6,1024]{3,2,1,0:T(8,128)(2,1)S(1)}, bf16[3,3,6,1024]{3,2,1,0:T(8,128)(2,1)S(1)}, u32[]{:S(2)}, u32[]{:S(2)}) collective-permute-start(bf16[3,3,6,1024]{3,2,1,0:T(8,128)(2,1)S(1)} %slice.93), channel_id=1, source_target_pairs={{0,6},{2,0},{4,2},{6,4},{1,7},{3,1},{5,3},{7,5},{8,14},{10,8},{12,... | collective-permute-start | bytes 331784 | tf_op jit(solution)/shard_map/ppermute | solution.py:209
  86.6 10.1 %collective-permute-start.5 = (bf16[3,3,24,1024]{3,2,1,0:T(8,128)(2,1)S(1)}, bf16[3,3,24,1024]{3,2,1,0:T(8,128)(2,1)S(1)}, u32[]{:S(2)}, u32[]{:S(2)}) collective-permute-start(bf16[3,3,24,1024]{3,2,1,0:T(8,128)(2,1)S(1)} %get-tuple-element.16), channel_id=1, source_target_pairs={{0,120},{8,16},{16,8},{24,32},{32,24},{40,48},{48,40},{56,64},{64,... | collective-permute-start | bytes 1327112 | tf_op jit(solution)/shard_map/ppermute | solution.py:215
  117.6 9.9 %collective-permute-start.6 = (bf16[3,3,24,1024]{3,2,1,0:T(8,128)(2,1)S(1)}, bf16[3,3,24,1024]{3,2,1,0:T(8,128)(2,1)S(1)}, u32[]{:S(2)}, u32[]{:S(2)}) collective-permute-start(bf16[3,3,24,1024]{3,2,1,0:T(8,128)(2,1)S(1)} %slice.94), channel_id=1, source_target_pairs={{0,120},{8,16},{16,8},{24,32},{32,24},{40,48},{48,40},{56,64},{64,... | collective-permute-start | bytes 1327112 | tf_op jit(solution)/shard_map/ppermute | solution.py:215
  128.7 6.4 %collective-permute-start.7 = (bf16[3,3,6,1024]{3,2,1,0:T(8,128)(2,1)S(1)}, bf16[3,3,6,1024]{3,2,1,0:T(8,128)(2,1)S(1)}, u32[]{:S(2)}, u32[]{:S(2)}) collective-permute-start(bf16[3,3,6,1024]{3,2,1,0:T(8,128)(2,1)S(1)} %slice.96), channel_id=1, source_target_pairs={{0,2},{2,4},{4,6},{6,0},{1,3},{3,5},{5,7},{7,1},{8,10},{10,12},{12... | collective-permute-start | bytes 331784 | tf_op jit(solution)/shard_map/ppermute | solution.py:209
  144.2 5.2 %collective-permute-start.8 = (bf16[3,6,6,512]{3,2,1,0:T(8,128)(2,1)S(1)}, bf16[3,6,6,512]{3,2,1,0:T(8,128)(2,1)S(1)}, u32[]{:S(2)}, u32[]{:S(2)}) collective-permute-start(bf16[3,6,6,512]{3,2,1,0:T(8,128)(2,1)S(1)} %slice.99), channel_id=1, source_target_pairs={{0,6},{2,0},{4,2},{6,4},{1,7},{3,1},{5,3},{7,5},{8,14},{10,8},{12,... | collective-permute-start | bytes 331784 | tf_op jit(solution)/shard_map/ppermute | solution.py:209
  149.6 10.9 %collective-permute-start.9 = (bf16[3,3,96,512]{3,2,1,0:T(8,128)(2,1)S(1)}, bf16[3,3,96,512]{3,2,1,0:T(8,128)(2,1)S(1)}, u32[]{:S(2)}, u32[]{:S(2)}) collective-permute-start(bf16[3,3,96,512]{3,2,1,0:T(8,128)(2,1)S(1)} %get-tuple-element.6), channel_id=1, source_target_pairs={{0,120},{8,0},{16,8},{24,16},{32,24},{40,32},{48,40},{56,48},{64,5... | collective-permute-start | bytes 2654216 | tf_op jit(solution)/shard_map/ppermute | solution.py:209
  188.4 14.8 %collective-permute-start.10 = (bf16[3,3,96,512]{3,2,1,0:T(8,128)(2,1)S(1)}, bf16[3,3,96,512]{3,2,1,0:T(8,128)(2,1)S(1)}, u32[]{:S(2)}, u32[]{:S(2)}) collective-permute-start(bf16[3,3,96,512]{3,2,1,0:T(8,128)(2,1)S(1)} %get-tuple-element.9), channel_id=1, source_target_pairs={{0,8},{8,16},{16,24},{24,32},{32,40},{40,48},{48,56},{56,64},{64,7... | collective-permute-start | bytes 2654216 | tf_op jit(solution)/shard_map/ppermute | solution.py:209
  203.2 6.4 %collective-permute-start.11 = (bf16[3,6,6,512]{3,2,1,0:T(8,128)(2,1)S(1)}, bf16[3,6,6,512]{3,2,1,0:T(8,128)(2,1)S(1)}, u32[]{:S(2)}, u32[]{:S(2)}) collective-permute-start(bf16[3,6,6,512]{3,2,1,0:T(8,128)(2,1)S(1)} %pad_maximum_fusion.8), channel_id=1, source_target_pairs={{0,2},{2,4},{4,6},{6,0},{1,3},{3,5},{5,7},{7,1},{8,10},{10,12},{12... | collective-permute-start | bytes 331784 | tf_op jit(solution)/shard_map/ppermute | solution.py:209
where the time goes:
time: 212 us
  waiting for transfers between devices  91.9 us (43%)
  Pallas kernels  82.5 us (39%)
  starting transfers between devices  13 us (6%)
  local copies, waits for them, and re-layouts  12.9 us (6%)
  other arithmetic  11.2 us (5%)
    ppermute x10, waiting for transfers between devices, shift(): lax.ppermute(value, axis, [(s, (s + steps) % count) for s in range(count)])  72.3 us
    pallas_call x2, Pallas kernels, fine_call(): pl.pallas_call(fine_kernel, out_shape=jax.ShapeDtypeStruct(x.shape, bf16)...  50 us
    ppermute x2, waiting for transfers between devices, swap_band(): return lax.ppermute(value, 'lat', pairs)  19.6 us
    pallas_call x1, Pallas kernels, coarse_call(): pl.pallas_call(coarse_kernel, out_shape=jax.ShapeDtypeStruct(x.shape, bf1...  18.9 us
    ppermute x10, starting transfers between devices, shift(): lax.ppermute(value, axis, [(s, (s + steps) % count) for s in range(count)])  12.7 us
    pallas_call x1, Pallas kernels, split_call(): pl.pallas_call(split_kernel, out_shape=jax.ShapeDtypeStruct(x.shape, bf16...  6.95 us
    pallas_call x1, Pallas kernels, merge_call(): pl.pallas_call(merge_kernel, out_shape=jax.ShapeDtypeStruct((3, 3, 48, 10...  6.63 us
    slice x2, local copies, waits for them, and re-layouts, roll_ahead(): field[:, :, 6:]  4.53 us
  transfers between devices with their start and end apart: 12, of which 12 were waited for; matrix products, arithmetic and copies ran while one was open for 3% of the time, Pallas kernels for 0%

commit v1 on v0

v1 whole, which is shorter than its diff:
```python
import jax
import jax.numpy as jnp
from jax import lax
from jax.experimental import pallas as pl
from jax.experimental.pallas import tpu as pltpu
from jax.sharding import PartitionSpec as P

NT = (((1,), (1,)), ((), ()))
TN = (((0,), (0,)), ((), ()))
f32 = jnp.float32
bf16 = jnp.bfloat16


def norm(x, g):
    c = jnp.mean(x, axis=-1, keepdims=True)
    d = x - c
    s = jnp.mean(d * d, axis=-1, keepdims=True)
    return (d * lax.rsqrt(s + 1e-05) * g).astype(bf16)


def attend_window(x, g, wqkv_ref, wvt_ref, wo_ref, qk_s, vt_s, ot_s, bias_ref):
    E = x.shape[1]
    h = norm(x, g)
    q = jnp.dot(h, wqkv_ref[:, :E], preferred_element_type=f32)
    qk_s[:, :E] = q.astype(bf16) * bf16(0.125)
    k = jnp.dot(h, wqkv_ref[:, E : 2 * E], preferred_element_type=f32)
    qk_s[:, E : 2 * E] = k.astype(bf16)
    vt = lax.dot_general(wvt_ref[...], h, NT, preferred_element_type=f32)
    vt_s[...] = vt.astype(bf16)
    lane = lax.broadcasted_iota(jnp.int32, (216, 128), 1)
    for hp in range(E // 128):
        qb = qk_s[:, 128 * hp : 128 * hp + 128]
        kb = qk_s[:, E + 128 * hp : E + 128 * hp + 128]
        for half in range(2):
            qm = jnp.where((lane >= 64) if half else (lane < 64), qb, bf16(0))
            st = lax.dot_general(kb, qm, NT, preferred_element_type=f32)
            if bias_ref is not None:
                st = st + bias_ref[...]
            m = jnp.max(st, axis=0, keepdims=True)
            e = jnp.exp(st - m)
            d = jnp.sum(e, axis=0, keepdims=True)
            hd = 64 * (2 * hp + half)
            ot = jnp.dot(vt_s[hd : hd + 64, :], e.astype(bf16), preferred_element_type=f32)
            ot_s[hd : hd + 64, :] = (ot * (1.0 / d)).astype(bf16)
    y = lax.dot_general(ot_s[...], wo_ref[...], TN, preferred_element_type=f32)
    return x + y


def token_label(t, lab_ref, start):
    t = t - jnp.where(t >= 144, 144, jnp.where(t >= 72, 72, 0))
    n = lab_ref.shape[0]
    out = jnp.zeros(t.shape, jnp.int32)
    for r in range(6):
        lab = lab_ref[lax.rem(start + r + n, n)]
        out = jnp.where(t >= 12 * r, lab, out)
    return out


def fill_bias(bias_ref, lab_ref, start):
    kt = token_label(lax.broadcasted_iota(jnp.int32, (216, 216), 0), lab_ref, start)
    qt = token_label(lax.broadcasted_iota(jnp.int32, (216, 216), 1), lab_ref, start)
    bias_ref[...] = jnp.where(kt == qt, f32(0), f32(-1e30))


def vm():
    return pl.BlockSpec(memory_space=pltpu.VMEM)


def mega_kernel(
    lab_ref, x_hbm, g1, w1_hbm, o1_hbm, mg, mw_hbm, gc, wc_hbm, oc_hbm, sg, sw_hbm, g3, w3_hbm, o3_hbm,
    out_ref,
    w1, o1, mw, wc, oc, sw, w3, o3, wvt, wvtc,
    xa, xb, xw, nbuf, ebuf, sedge, jbuf, redge, sedge2, comb, hedge, sedge3,
    hx, tmp, bias, qk_s, vt_s, ot_s, qkc, vtc, otc,
    wsem, own_s, own8_s, s0a, r0a, s0b, r0b, own8_r,
    s1, r1, s1e, r1e, s2, r2, s2e, r2e, s3, r3, s3e, r3e,
):
    i = lax.axis_index("lat")
    c = lax.axis_index("lon")
    n_lat = lax.axis_size("lat")
    n_lon = lax.axis_size("lon")
    o = lax.rem(i, 2)

    def dev(di, dc):
        return {"lat": lax.rem(i + di + n_lat, n_lat), "lon": lax.rem(c + dc + n_lon, n_lon)}

    def remote(src, dst, ssem, rsem, to):
        return pltpu.make_async_remote_copy(
            src_ref=src, dst_ref=dst, send_sem=ssem, recv_sem=rsem, device_id=to,
            device_id_type=pl.DeviceIdType.MESH,
        )

    own = pltpu.make_async_copy(
        x_hbm.at[:, :, pl.ds(pl.multiple_of(48 * (1 - o), 16), 48)], xa.at[:, 3:9], own_s
    )
    own.start()
    weights = [
        pltpu.make_async_copy(a, b, wsem.at[k])
        for k, (a, b) in enumerate(
            ((w1_hbm, w1), (o1_hbm, o1), (mw_hbm, mw), (wc_hbm, wc), (oc_hbm, oc), (sw_hbm, sw), (w3_hbm, w3), (o3_hbm, o3))
        )
    ]
    weights[0].start()
    weights[1].start()

    barrier = pltpu.get_barrier_semaphore()
    side = 1 - 2 * o
    for di, dc in ((-1, 0), (1, 0), (-2, 0), (2, 0), (0, -1), (0, 1), (-1, side), (1, side)):
        pl.semaphore_signal(barrier, inc=1, device_id=dev(di, dc), device_id_type=pl.DeviceIdType.MESH)
    pl.semaphore_wait(barrier, 8)

    def t0a(g):
        return remote(
            x_hbm.at[:, pl.ds(3 * g, 3), pl.ds(pl.multiple_of(48 * o, 16), 48)],
            xa.at[:, pl.ds(9 * (1 - g), 3)], s0a.at[1 - g], r0a.at[1 - g], dev(2 * g - 1, 0),
        )

    def t0b(g):
        return remote(
            x_hbm.at[:, pl.ds(3 * g, 3), pl.ds(pl.multiple_of(48 * (1 - o), 16), 8)],
            xb.at[:, pl.ds(9 * (1 - g), 3)], s0b.at[1 - g], r0b.at[1 - g], dev(2 * g - 1, -o),
        )

    def t0c_remote():
        return remote(x_hbm.at[:, :, 0:8], xb.at[:, 3:9], own8_s, own8_r, dev(0, -1))

    def t0c_local():
        return pltpu.make_async_copy(x_hbm.at[:, :, 48:56], xb.at[:, 3:9], own8_r)

    g_in = 1 - o
    for g in (0, 1):
        t0a(g).start()
        t0b(g).start()

    @pl.when(o == 0)
    def _():
        t0c_remote().start()

    @pl.when(o == 1)
    def _():
        t0c_local().start()

    for copy in weights[2:]:
        copy.start()

    fill_bias(bias.at[0], lab_ref, i * 6 - 3 + n_lat * 6)
    fill_bias(bias.at[1], lab_ref, i * 6 + 3)
    weights[0].wait()
    weights[1].wait()
    wvt[...] = w1[:, 1024:1536].T
    own.wait()

    @pl.when(o == 0)
    def _():
        t0c_remote().wait_recv()

    @pl.when(o == 1)
    def _():
        t0c_local().wait()

    fb = 3 * (1 - o)
    gb = 3 * o

    def chunk_to(k):
        far = jnp.where(o == 1, jnp.where(k == 0, -1, 1), jnp.where(k == 3, 1, -1))
        return lax.rem(k + 1 + 2 * o, 4), far

    def edge1(k):
        m, far = chunk_to(k)
        return remote(sedge.at[:, pl.ds(3 * k, 3)], ebuf.at[:, pl.ds(3 * m, 3)], s1e.at[k], r1e.at[m], dev(far, -o))

    def edge2(k):
        m, far = chunk_to(k)
        return remote(sedge2.at[:, pl.ds(3 * k, 3)], redge.at[:, pl.ds(3 * m, 3)], s2e.at[k], r2e.at[m], dev(far, 1 - o))

    rows1 = remote(
        nbuf.at[:, pl.ds(12 * (1 - o), 3)], nbuf.at[:, pl.ds(12 * o, 3)], s1, r1, dev(2 - 4 * o, 0)
    )
    rows2 = remote(
        jbuf.at[:, pl.ds(12 * o, 3)], jbuf.at[:, pl.ds(12 * (1 - o), 3)], s2, r2, dev(4 * o - 2, 0)
    )

    def group1(s, carry):
        g = (1 - o) * (1 - s) + o * s
        t0a(1 - g).wait_recv()
        t0b(1 - g).wait_recv()
        for lr in range(18):
            a = xa[lr // 6, 6 * g + lr % 6].astype(f32)
            b = xb[lr // 6, 6 * g + lr % 6].astype(f32)
            for w in range(3):
                xw[4 * g + w, 12 * lr : 12 * lr + 12, :] = a[6 + 12 * w : 18 + 12 * w]
            xw[4 * g + 3, 12 * lr : 12 * lr + 6, :] = a[42:48]
            xw[4 * g + 3, 12 * lr + 6 : 12 * lr + 12, :] = b[0:6]

        def window(w, carry):
            z = 4 * g + w
            xw[z] = attend_window(xw[z], g1[...], w1, wvt, o1, qk_s, vt_s, ot_s, bias.at[g])

            @pl.when(w == 0)
            def _():
                for lr in range(18):
                    sedge[lr // 6, 6 * g + lr % 6] = xw[z, 12 * lr : 12 * lr + 8, :].astype(bf16)
                edge1(2 * g).start()
                edge1(2 * g + 1).start()

            return carry

        lax.fori_loop(0, 4, window, 0)
        for lr in range(18):
            slab = jnp.concatenate([xw[4 * g + w, 12 * lr : 12 * lr + 12, :] for w in range(4)], axis=0)
            nbuf[lr // 6, fb + 6 * g + lr % 6] = slab.astype(bf16)

        @pl.when(s == 0)
        def _():
            rows1.start()

        return carry

    lax.fori_loop(0, 2, group1, 0)

    for copy in weights[2:6]:
        copy.wait()
    wvtc[...] = wc[:, 2048:3072].T
    rows1.wait_recv()
    for k in range(4):
        edge1(k).wait_recv()
    for lr in range(18):
        l, rr = lr // 6, lr % 6
        for r in range(2):
            a = nbuf[l, gb + 2 * rr + r].astype(f32)
            b = ebuf[l, 2 * rr + r].astype(f32)
            for j in range(4):
                tmp[r, j, 0:48] = a[:, 128 * j : 128 * j + 128]
                tmp[r, j, 48:56] = b[:, 128 * j : 128 * j + 128]
        for p in range(4):
            for j in range(4):
                v = tmp[p % 2, j, pl.ds(6 + p // 2, 24, stride=2), :]
                col = 512 * p + 128 * j
                for w in range(2):
                    hx[w, 12 * lr : 12 * lr + 12, col : col + 128] = v[12 * w : 12 * w + 12]

    def coarse(w, carry):
        merged = jnp.dot(norm(hx[w], mg[...]), mw[...], preferred_element_type=f32)
        x = merged.astype(bf16).astype(f32)
        y = attend_window(x, gc[...], wc, wvtc, oc, qkc, vtc, otc, None)
        h = norm(y.astype(bf16).astype(f32), sg[...])
        hx[w] = jnp.dot(h, sw[...], preferred_element_type=f32)
        return carry

    lax.fori_loop(0, 2, coarse, 0)
    for lr in range(18):
        l, rr = lr // 6, lr % 6
        for p in range(4):
            for j in range(4):
                col = 512 * p + 128 * j
                v = jnp.concatenate([hx[w, 12 * lr : 12 * lr + 12, col : col + 128] for w in range(2)], axis=0)
                tmp[p % 2, j, pl.ds(6 + p // 2, 24, stride=2), :] = v
        for r in range(2):
            sp = jnp.concatenate([tmp[r, j] for j in range(4)], axis=1)
            a = nbuf[l, gb + 2 * rr + r].astype(f32)
            b = ebuf[l, 2 * rr + r].astype(f32)
            jbuf[l, gb + 2 * rr + r] = (a + sp[0:48]).astype(bf16)
            sedge2[l, 2 * rr + r] = (b + sp[48:56]).astype(bf16)
    for k in range(4):
        edge2(k).start()
    rows2.start()

    weights[6].wait()
    weights[7].wait()
    wvt[...] = w3[:, 1024:1536].T

    def t3(g):
        return remote(
            comb.at[1 - o, :, pl.ds(9 * g, 3)], comb.at[1 - o, :, pl.ds(6 - 3 * g, 3)], s3.at[g], r3.at[1 - g],
            dev(2 * g - 1, 0),
        )

    def edge3(k):
        far = jnp.where(k == 0, -1, jnp.where(k == 3, 1, 0))
        m = lax.rem(k + 1, 2)
        return remote(sedge3.at[:, pl.ds(3 * k, 3)], hedge.at[:, pl.ds(3 * m, 3)], s3e.at[k], r3e.at[m], dev(far, 1))

    def group3(s, carry):
        g = o * (1 - s) + (1 - o) * s

        def landed(k, carry):
            m = 2 * g + k
            remote(sedge2.at[:, pl.ds(0, 3)], redge.at[:, pl.ds(3 * m, 3)], s2e.at[0], r2e.at[m], dev(1, 0)).wait_recv()
            return carry

        lax.fori_loop(0, 2, landed, 0)

        @pl.when(s == 1)
        def _():
            rows2.wait_recv()

        for lr in range(18):
            a = jbuf[lr // 6, fb + 6 * g + lr % 6].astype(f32)
            b = redge[lr // 6, 6 * g + lr % 6].astype(f32)
            xw[4 * g, 12 * lr : 12 * lr + 6, :] = b[0:6]
            xw[4 * g, 12 * lr + 6 : 12 * lr + 12, :] = a[6:12]
            for w in range(1, 4):
                xw[4 * g + w, 12 * lr : 12 * lr + 12, :] = a[12 * w : 12 * w + 12]

        def window(w, carry):
            z = 4 * g + w
            xw[z] = attend_window(xw[z], g3[...], w3, wvt, o3, qk_s, vt_s, ot_s, bias.at[g])
            return carry

        lax.fori_loop(0, 4, window, 0)
        for lr in range(18):
            sedge3[lr // 6, 6 * g + lr % 6] = xw[4 * g + 3, 12 * lr + 4 : 12 * lr + 12, :].astype(bf16)

        @pl.when(o == 0)
        def _():
            edge3(2 * g).start()
            edge3(2 * g + 1).start()

        for lr in range(18):
            slab = jnp.concatenate([xw[4 * g + w, 12 * lr : 12 * lr + 12, :] for w in range(4)], axis=0)
            comb[1 - o, lr // 6, 6 * g + lr % 6] = slab.astype(bf16)
        t3(g).start()
        return carry

    lax.fori_loop(0, 2, group3, 0)

    for g in (0, 1):
        remote(
            comb.at[o, :, pl.ds(0, 3)], comb.at[o, :, pl.ds(3 + 3 * g, 3)], s3.at[g], r3.at[g], dev(1, 0)
        ).wait_recv()
        remote(sedge3.at[:, pl.ds(0, 3)], hedge.at[:, pl.ds(3 * g, 3)], s3e.at[g], r3e.at[g], dev(0, 1)).wait_recv()
    for lr in range(18):
        l, r = lr // 6, lr % 6
        e = hedge[l, r].astype(f32)
        left = comb[0, l, r + 3].astype(f32)
        right = comb[1, l, r + 3].astype(f32)
        out_ref[l, r] = jnp.concatenate([e[2:8], left, right[0:42]], axis=0).astype(bf16)

    for g in (0, 1):
        t0a(1 - g).wait_send()
        t0b(1 - g).wait_send()
        t3(g).wait_send()
    for k in range(4):
        edge1(k).wait_send()
        edge2(k).wait_send()
    rows1.wait_send()
    rows2.wait_send()

    @pl.when(o == 0)
    def _():
        t0c_remote().wait_send()
        for k in range(4):
            edge3(k).wait_send()


def mega_call(x, lab, g1, w1, o1, mg, mw, gc, wc, oc, sg, sw, g3, w3, o3):
    V = vm()
    H = pl.BlockSpec(memory_space=pl.ANY)
    B = lambda *s: pltpu.VMEM(s, bf16)
    F = lambda *s: pltpu.VMEM(s, f32)
    D = pltpu.SemaphoreType.DMA
    weights = [B(*a.shape) for a in (w1, o1, mw, wc, oc, sw, w3, o3)]
    scratch = weights + [
        B(512, 512), B(1024, 1024),
        B(3, 12, 48, 512), B(3, 12, 8, 512), F(8, 216, 512), B(3, 15, 48, 512), B(3, 12, 8, 512), B(3, 12, 8, 512),
        B(3, 15, 48, 512), B(3, 12, 8, 512), B(3, 12, 8, 512), B(2, 3, 12, 48, 512), B(3, 6, 8, 512), B(3, 12, 8, 512),
        F(2, 216, 2048), F(2, 4, 56, 128), F(2, 216, 216), B(216, 1024), B(512, 216), B(512, 216),
        B(216, 2048), B(1024, 216), B(1024, 216),
        D((8,)), D, D, D((2,)), D((2,)), D((2,)), D((2,)), D,
        D, D, D((4,)), D((4,)), D, D, D((4,)), D((4,)), D((2,)), D((2,)), D((4,)), D((2,)),
    ]
    row = lambda g: g.reshape(1, -1)
    return pl.pallas_call(
        mega_kernel,
        out_shape=jax.ShapeDtypeStruct(x.shape, bf16),
        in_specs=[pl.BlockSpec(memory_space=pltpu.SMEM), H, V, H, H, V, H, V, H, H, V, H, V, H, H],
        out_specs=V,
        scratch_shapes=scratch,
        compiler_params=pltpu.CompilerParams(
            vmem_limit_bytes=67043328, collective_id=0, has_side_effects=True
        ),
        name="section",
    )(lab, x, row(g1), w1, o1, row(mg), mw, row(gc), wc, oc, row(sg), sw, row(g3), w3, o3)


def solution(mesh):
    return jax.shard_map(
        mega_call,
        mesh=mesh,
        in_specs=(P("rep", "lat", "lon", None),) + (P(),) * 14,
        out_specs=P("rep", "lat", "lon", None),
        check_vma=False,
    )
```

time: 212 us -> 87.6 us (0.41)
  the two profiles are of different devices: /device:TPU:0 before, /device:TPU:1 now
where the time goes in v1:
time: 87.6 us; the launch traced here: 87.5 us
  Pallas kernels  84.6 us (97%)
  local copies, waits for them, and re-layouts  2.84 us (3%)
    pallas_call x1, Pallas kernels, mega_call(): pl.pallas_call(mega_kernel, out_shape=jax.ShapeDtypeStruct(x.shape, bf16)...  84.6 us
    unnamed x1, local copies, waits for them, and re-layouts  2.84 us

profile of v1, /device:TPU:1, one launch (start us, length us, event | category | flops | bytes accessed | tf_op | source)
XLA Modules:
  0.0 87.5 jit_solution(13681936095228612785)
XLA Ops:
  0.0 84.6 %section.1 = bf16[3,6,96,512]{3,2,1,0:T(8,128)(2,1)} custom-call(s32[96]{0:T(128)} %lab_ref.1, bf16[3,6,96,512]{3,2,1,0:T(8,128)(2,1)} %x_hbm.1, f32[1,512]{1,0:T(1,128)} %bitcast.8, bf16[512,1536]{1,0:T(8,128)(2,1)} %w1_hbm.1, bf16[512,512]{1,0:T(8,128)(2,1)} %o1_hbm.1, f32[1,2048]{1,0:T(1,128)} %bitcast.5, bf16[2048,1024]{1,0:T(8,128)(2,1)} %mw_hbm.1, ...), custom_call_target="tpu_custom_call" | custom-call | tf_op jit(solution)/shard_map/section/pallas_call | solution.py:373
  84.6 2.8 %copy.17 = bf16[3,6,96,512]{3,2,1,0:T(8,128)(2,1)} copy(bf16[3,6,96,512]{3,2,1,0:T(8,128)(2,1)} %section.1) | data formatting | bytes 3538944

commit v2 on v1

--- a/solution.py
+++ b/solution.py
@@ -18,32 +18,46 @@
     return (d * lax.rsqrt(s + 1e-05) * g).astype(bf16)
 
 
-def attend_window(x, g, wqkv_ref, wvt_ref, wo_ref, qk_s, vt_s, ot_s, bias_ref):
-    E = x.shape[1]
-    h = norm(x, g)
-    q = jnp.dot(h, wqkv_ref[:, :E], preferred_element_type=f32)
-    qk_s[:, :E] = q.astype(bf16) * bf16(0.125)
-    k = jnp.dot(h, wqkv_ref[:, E : 2 * E], preferred_element_type=f32)
-    qk_s[:, E : 2 * E] = k.astype(bf16)
-    vt = lax.dot_general(wvt_ref[...], h, NT, preferred_element_type=f32)
-    vt_s[...] = vt.astype(bf16)
+def attend_windows(n, load, finish, g, wqkv_ref, wvt_ref, wo_ref, qk_s, vt_s, ot_s, bias_ref):
+    E = wqkv_ref.shape[0]
+    heads = E // 64
+    for t in range(n):
+        h = norm(load(t), g)
+        q = jnp.dot(h, wqkv_ref[:, :E], preferred_element_type=f32)
+        qk_s[t, :, :E] = (q * 0.125).astype(bf16)
+        k = jnp.dot(h, wqkv_ref[:, E : 2 * E], preferred_element_type=f32)
+        qk_s[t, :, E : 2 * E] = k.astype(bf16)
+        vt = lax.dot_general(wvt_ref[...], h, NT, preferred_element_type=f32)
+        vt_s[t] = vt.astype(bf16)
     lane = lax.broadcasted_iota(jnp.int32, (216, 128), 1)
-    for hp in range(E // 128):
-        qb = qk_s[:, 128 * hp : 128 * hp + 128]
-        kb = qk_s[:, E + 128 * hp : E + 128 * hp + 128]
-        for half in range(2):
-            qm = jnp.where((lane >= 64) if half else (lane < 64), qb, bf16(0))
-            st = lax.dot_general(kb, qm, NT, preferred_element_type=f32)
-            if bias_ref is not None:
-                st = st + bias_ref[...]
-            m = jnp.max(st, axis=0, keepdims=True)
-            e = jnp.exp(st - m)
-            d = jnp.sum(e, axis=0, keepdims=True)
-            hd = 64 * (2 * hp + half)
-            ot = jnp.dot(vt_s[hd : hd + 64, :], e.astype(bf16), preferred_element_type=f32)
-            ot_s[hd : hd + 64, :] = (ot * (1.0 / d)).astype(bf16)
-    y = lax.dot_general(ot_s[...], wo_ref[...], TN, preferred_element_type=f32)
-    return x + y
+
+    def scores(t, h):
+        hp = h // 2
+        qb = qk_s[t, :, 128 * hp : 128 * hp + 128]
+        kb = qk_s[t, :, E + 128 * hp : E + 128 * hp + 128]
+        qm = jnp.where((lane >= 64) if h % 2 else (lane < 64), qb, bf16(0))
+        st = lax.dot_general(kb, qm, NT, preferred_element_type=f32)
+        return st if bias_ref is None else st + bias_ref[...]
+
+    def mix(t, h, e, d):
+        ot = jnp.dot(vt_s[t, 64 * h : 64 * h + 64, :], e, preferred_element_type=f32)
+        ot_s[t, 64 * h : 64 * h + 64, :] = (ot * d).astype(bf16)
+        if h == heads - 1:
+            finish(t, lax.dot_general(ot_s[t], wo_ref[...], TN, preferred_element_type=f32))
+
+    items = [(t, h) for t in range(n) for h in range(heads)]
+    ready = [scores(*it) for it in items[:2]]
+    waiting = []
+    for k, it in enumerate(items):
+        if k + 2 < len(items):
+            ready.append(scores(*items[k + 2]))
+        st = ready.pop(0)
+        e = jnp.exp(st - jnp.max(st, axis=0, keepdims=True))
+        waiting.append((*it, e.astype(bf16), 1.0 / jnp.sum(e, axis=0, keepdims=True)))
+        if len(waiting) > 2:
+            mix(*waiting.pop(0))
+    for args in waiting:
+        mix(*args)
 
 
 def token_label(t, lab_ref, start):
@@ -71,7 +85,7 @@
     out_ref,
     w1, o1, mw, wc, oc, sw, w3, o3, wvt, wvtc,
     xa, xb, xw, nbuf, ebuf, sedge, jbuf, redge, sedge2, comb, hedge, sedge3,
-    hx, tmp, bias, qk_s, vt_s, ot_s, qkc, vtc, otc,
+    hx, xc, tmp, bias, qk_s, vt_s, ot_s, qkc, vtc, otc,
     wsem, own_s, own8_s, s0a, r0a, s0b, r0b, own8_r,
     s1, r1, s1e, r1e, s2, r2, s2e, r2e, s3, r3, s3e, r3e,
 ):
@@ -192,20 +206,15 @@
             xw[4 * g + 3, 12 * lr : 12 * lr + 6, :] = a[42:48]
             xw[4 * g + 3, 12 * lr + 6 : 12 * lr + 12, :] = b[0:6]
 
-        def window(w, carry):
-            z = 4 * g + w
-            xw[z] = attend_window(xw[z], g1[...], w1, wvt, o1, qk_s, vt_s, ot_s, bias.at[g])
-
-            @pl.when(w == 0)
-            def _():
+        def finish(t, y):
+            xw[4 * g + t] = xw[4 * g + t] + y
+            if t == 0:
                 for lr in range(18):
-                    sedge[lr // 6, 6 * g + lr % 6] = xw[z, 12 * lr : 12 * lr + 8, :].astype(bf16)
+                    sedge[lr // 6, 6 * g + lr % 6] = xw[4 * g, 12 * lr : 12 * lr + 8, :].astype(bf16)
                 edge1(2 * g).start()
                 edge1(2 * g + 1).start()
 
-            return carry
-
-        lax.fori_loop(0, 4, window, 0)
+        attend_windows(4, lambda t: xw[4 * g + t], finish, g1[...], w1, wvt, o1, qk_s, vt_s, ot_s, bias.at[g])
         for lr in range(18):
             slab = jnp.concatenate([xw[4 * g + w, 12 * lr : 12 * lr + 12, :] for w in range(4)], axis=0)
             nbuf[lr // 6, fb + 6 * g + lr % 6] = slab.astype(bf16)
@@ -239,15 +248,16 @@
                 for w in range(2):
                     hx[w, 12 * lr : 12 * lr + 12, col : col + 128] = v[12 * w : 12 * w + 12]
 
-    def coarse(w, carry):
-        merged = jnp.dot(norm(hx[w], mg[...]), mw[...], preferred_element_type=f32)
-        x = merged.astype(bf16).astype(f32)
-        y = attend_window(x, gc[...], wc, wvtc, oc, qkc, vtc, otc, None)
-        h = norm(y.astype(bf16).astype(f32), sg[...])
+    def merged(w):
+        m = jnp.dot(norm(hx[w], mg[...]), mw[...], preferred_element_type=f32)
+        xc[w] = m.astype(bf16).astype(f32)
+        return xc[w]
+
+    def split(w, y):
+        h = norm((xc[w] + y).astype(bf16).astype(f32), sg[...])
         hx[w] = jnp.dot(h, sw[...], preferred_element_type=f32)
-        return carry
-
-    lax.fori_loop(0, 2, coarse, 0)
+
+    attend_windows(2, merged, split, gc[...], wc, wvtc, oc, qkc, vtc, otc, None)
     for lr in range(18):
         l, rr = lr // 6, lr % 6
         for p in range(4):
@@ -302,12 +312,10 @@
             for w in range(1, 4):
                 xw[4 * g + w, 12 * lr : 12 * lr + 12, :] = a[12 * w : 12 * w + 12]
 
-        def window(w, carry):
-            z = 4 * g + w
-            xw[z] = attend_window(xw[z], g3[...], w3, wvt, o3, qk_s, vt_s, ot_s, bias.at[g])
-            return carry
-
-        lax.fori_loop(0, 4, window, 0)
+        def finish(t, y):
+            xw[4 * g + t] = xw[4 * g + t] + y
+
+        attend_windows(4, lambda t: xw[4 * g + t], finish, g3[...], w3, wvt, o3, qk_s, vt_s, ot_s, bias.at[g])
         for lr in range(18):
             sedge3[lr // 6, 6 * g + lr % 6] = xw[4 * g + 3, 12 * lr + 4 : 12 * lr + 12, :].astype(bf16)
 
@@ -364,8 +372,8 @@
         B(512, 512), B(1024, 1024),
         B(3, 12, 48, 512), B(3, 12, 8, 512), F(8, 216, 512), B(3, 15, 48, 512), B(3, 12, 8, 512), B(3, 12, 8, 512),
         B(3, 15, 48, 512), B(3, 12, 8, 512), B(3, 12, 8, 512), B(2, 3, 12, 48, 512), B(3, 6, 8, 512), B(3, 12, 8, 512),
-        F(2, 216, 2048), F(2, 4, 56, 128), F(2, 216, 216), B(216, 1024), B(512, 216), B(512, 216),
-        B(216, 2048), B(1024, 216), B(1024, 216),
+        F(2, 216, 2048), F(2, 216, 1024), F(2, 4, 56, 128), F(2, 216, 216), B(4, 216, 1024), B(4, 512, 216), B(4, 512, 216),
+        B(2, 216, 2048), B(2, 1024, 216), B(2, 1024, 216),
         D((8,)), D, D, D((2,)), D((2,)), D((2,)), D((2,)), D,
         D, D, D((4,)), D((4,)), D, D, D((4,)), D((4,)), D((2,)), D((2,)), D((4,)), D((2,)),
     ]

time: 87.6 us -> 67.3 us (0.77); the launches traced: 87.5 us -> 66.2 us
  Pallas kernels: 84.6 us -> 63.4 us
    pallas_call x1, Pallas kernels: 84.6 us -> 63.4 us  [mega_call(): pl.pallas_call(mega_kernel, out_shape=jax.ShapeDtypeStruct(x.shape, bf16)...]
where the time goes in v2:
time: 67.3 us; the launch traced here: 66.2 us
  Pallas kernels  63.4 us (94%)
  local copies, waits for them, and re-layouts  2.84 us (4%)
    pallas_call x1, Pallas kernels, mega_call(): pl.pallas_call(mega_kernel, out_shape=jax.ShapeDtypeStruct(x.shape, bf16)...  63.4 us
    unnamed x1, local copies, waits for them, and re-layouts  2.84 us

profile of v2, /device:TPU:1, one launch (start us, length us, event | category | flops | bytes accessed | tf_op | source)
XLA Modules:
  0.0 66.2 jit_solution(14264681889146246329)
XLA Ops:
  0.0 63.4 %section.1 = bf16[3,6,96,512]{3,2,1,0:T(8,128)(2,1)} custom-call(s32[96]{0:T(128)} %lab_ref.1, bf16[3,6,96,512]{3,2,1,0:T(8,128)(2,1)} %x_hbm.1, f32[1,512]{1,0:T(1,128)} %bitcast.8, bf16[512,1536]{1,0:T(8,128)(2,1)} %w1_hbm.1, bf16[512,512]{1,0:T(8,128)(2,1)} %o1_hbm.1, f32[1,2048]{1,0:T(1,128)} %bitcast.5, bf16[2048,1024]{1,0:T(8,128)(2,1)} %mw_hbm.1, ...), custom_call_target="tpu_custom_call" | custom-call | tf_op jit(solution)/shard_map/section/pallas_call | solution.py:381
  63.4 2.8 %copy.17 = bf16[3,6,96,512]{3,2,1,0:T(8,128)(2,1)} copy(bf16[3,6,96,512]{3,2,1,0:T(8,128)(2,1)} %section.1) | data formatting | bytes 3538944

commit v3 on v2

--- a/solution.py
+++ b/solution.py
@@ -1,3 +1,4 @@
+import functools
 import jax
 import jax.numpy as jnp
 from jax import lax
@@ -18,46 +19,77 @@
     return (d * lax.rsqrt(s + 1e-05) * g).astype(bf16)
 
 
-def attend_windows(n, load, finish, g, wqkv_ref, wvt_ref, wo_ref, qk_s, vt_s, ot_s, bias_ref):
+LOG2E = 1.4426950408889634
+
+
+def attend_windows(order, begin, finish, hold, g, wqkv_ref, wvt_ref, wo_ref, q_s, k_s, vt_s, ot_s, bias_ref):
     E = wqkv_ref.shape[0]
     heads = E // 64
-    for t in range(n):
-        h = norm(load(t), g)
-        q = jnp.dot(h, wqkv_ref[:, :E], preferred_element_type=f32)
-        qk_s[t, :, :E] = (q * 0.125).astype(bf16)
-        k = jnp.dot(h, wqkv_ref[:, E : 2 * E], preferred_element_type=f32)
-        qk_s[t, :, E : 2 * E] = k.astype(bf16)
-        vt = lax.dot_general(wvt_ref[...], h, NT, preferred_element_type=f32)
-        vt_s[t] = vt.astype(bf16)
-    lane = lax.broadcasted_iota(jnp.int32, (216, 128), 1)
+    lane = lax.broadcasted_iota(jnp.int32, (256, 128), 1)
+
+    def steps_of(t):
+        def normed():
+            hold[t] = norm(hold[t], g)
+
+        def query(c):
+            y = jnp.dot(hold[t], wqkv_ref[:, c : c + 256], preferred_element_type=f32)
+            q_s[t, :216, c : c + 256] = (y * (0.125 * LOG2E)).astype(bf16)
+
+        def key(c):
+            y = jnp.dot(hold[t], wqkv_ref[:, E + c : E + c + 256], preferred_element_type=f32)
+            k_s[t, :216, c : c + 256] = y.astype(bf16)
+
+        def value(c):
+            y = lax.dot_general(wvt_ref[c : c + 256, :], hold[t], NT, preferred_element_type=f32).astype(bf16)
+            for h in range(4):
+                vt_s[t, c // 64 + h, :64, :216] = y[64 * h : 64 * h + 64]
+
+        steps = list(begin(t)) + [normed]
+        for c in range(0, E, 256):
+            steps += [functools.partial(f, c) for f in (query, key, value)]
+        return steps
 
     def scores(t, h):
-        hp = h // 2
-        qb = qk_s[t, :, 128 * hp : 128 * hp + 128]
-        kb = qk_s[t, :, E + 128 * hp : E + 128 * hp + 128]
-        qm = jnp.where((lane >= 64) if h % 2 else (lane < 64), qb, bf16(0))
-        st = lax.dot_general(kb, qm, NT, preferred_element_type=f32)
+        hp = 128 * (h // 2)
+        qm = jnp.where((lane >= 64) if h % 2 else (lane < 64), q_s[t, :, hp : hp + 128], bf16(0))
+        st = lax.dot_general(k_s[t, :, hp : hp + 128], qm, NT, preferred_element_type=f32)[:216]
         return st if bias_ref is None else st + bias_ref[...]
 
-    def mix(t, h, e, d):
-        ot = jnp.dot(vt_s[t, 64 * h : 64 * h + 64, :], e, preferred_element_type=f32)
-        ot_s[t, 64 * h : 64 * h + 64, :] = (ot * d).astype(bf16)
+    def mix(t, h, e):
+        ot = jnp.dot(vt_s[t, h], e, preferred_element_type=f32)
+        ot_s[t, 64 * h : 64 * h + 64, :] = (ot[:64] * (1.0 / ot[64:65])).astype(bf16)[:, :216]
         if h == heads - 1:
-            finish(t, lax.dot_general(ot_s[t], wo_ref[...], TN, preferred_element_type=f32))
-
-    items = [(t, h) for t in range(n) for h in range(heads)]
-    ready = [scores(*it) for it in items[:2]]
-    waiting = []
-    for k, it in enumerate(items):
-        if k + 2 < len(items):
-            ready.append(scores(*items[k + 2]))
+            return finish(t, lax.dot_general(ot_s[t], wo_ref[...], TN, preferred_element_type=f32)) or []
+        return []
+
+    items = [(t, h) for t in order for h in range(heads)]
+    for step in steps_of(order[0]):
+        step()
+    ready = [scores(*it) for it in items[:3]]
+    waiting, later = [], []
+    for k, (t, h) in enumerate(items):
+        if h == 0:
+            place = order.index(t) + 1
+            todo = steps_of(order[place]) if place < len(order) else []
+        if h < heads - 3:
+            count = -(-len(todo) // (heads - 3 - h))
+            for step in todo[:count]:
+                step()
+            todo = todo[count:]
+        for step in later[:2]:
+            step()
+        later = later[2:]
+        if k + 3 < len(items):
+            ready.append(scores(*items[k + 3]))
         st = ready.pop(0)
-        e = jnp.exp(st - jnp.max(st, axis=0, keepdims=True))
-        waiting.append((*it, e.astype(bf16), 1.0 / jnp.sum(e, axis=0, keepdims=True)))
-        if len(waiting) > 2:
-            mix(*waiting.pop(0))
+        e = jnp.exp2(st - jnp.max(st, axis=0, keepdims=True))
+        waiting.append((t, h, jnp.concatenate([e, jnp.zeros((40, 256), f32)], axis=0).astype(bf16)))
+        if len(waiting) > 3:
+            later += mix(*waiting.pop(0))
     for args in waiting:
-        mix(*args)
+        later += mix(*args)
+    for step in later:
+        step()
 
 
 def token_label(t, lab_ref, start):
@@ -71,8 +103,8 @@
 
 
 def fill_bias(bias_ref, lab_ref, start):
-    kt = token_label(lax.broadcasted_iota(jnp.int32, (216, 216), 0), lab_ref, start)
-    qt = token_label(lax.broadcasted_iota(jnp.int32, (216, 216), 1), lab_ref, start)
+    kt = token_label(lax.broadcasted_iota(jnp.int32, (216, 256), 0), lab_ref, start)
+    qt = token_label(lax.broadcasted_iota(jnp.int32, (216, 256), 1), lab_ref, start)
     bias_ref[...] = jnp.where(kt == qt, f32(0), f32(-1e30))
 
 
@@ -85,9 +117,9 @@
     out_ref,
     w1, o1, mw, wc, oc, sw, w3, o3, wvt, wvtc,
     xa, xb, xw, nbuf, ebuf, sedge, jbuf, redge, sedge2, comb, hedge, sedge3,
-    hx, xc, tmp, bias, qk_s, vt_s, ot_s, qkc, vtc, otc,
+    hx, xc, tmp, etmp, bias, q_s, k_s, vt_s, ot_s, qc, kc, vtc, otc, final,
     wsem, own_s, own8_s, s0a, r0a, s0b, r0b, own8_r,
-    s1, r1, s1e, r1e, s2, r2, s2e, r2e, s3, r3, s3e, r3e,
+    s1, r1, s1e, r1e, s2, r2, s2e, r2e, s3, r3, s3e, r3e, osem,
 ):
     i = lax.axis_index("lat")
     c = lax.axis_index("lon")
@@ -157,6 +189,10 @@
     for copy in weights[2:]:
         copy.start()
 
+    for v in (vt_s, vtc):
+        n, heads = v.shape[:2]
+        v[:, :, 64:80, :] = jnp.ones((n, heads, 16, 256), bf16)
+        v[:, :, :64, 128:256] = jnp.zeros((n, heads, 64, 128), bf16)
     fill_bias(bias.at[0], lab_ref, i * 6 - 3 + n_lat * 6)
     fill_bias(bias.at[1], lab_ref, i * 6 + 3)
     weights[0].wait()
@@ -214,7 +250,15 @@
                 edge1(2 * g).start()
                 edge1(2 * g + 1).start()
 
-        attend_windows(4, lambda t: xw[4 * g + t], finish, g1[...], w1, wvt, o1, qk_s, vt_s, ot_s, bias.at[g])
+        hold = {}
+
+        def begin(t):
+            def take():
+                hold[t] = xw[4 * g + t]
+
+            return [take]
+
+        attend_windows([0, 1, 2, 3], begin, finish, hold, g1[...], w1, wvt, o1, q_s, k_s, vt_s, ot_s, bias.at[g])
         for lr in range(18):
             slab = jnp.concatenate([xw[4 * g + w, 12 * lr : 12 * lr + 12, :] for w in range(4)], axis=0)
             nbuf[lr // 6, fb + 6 * g + lr % 6] = slab.astype(bf16)
@@ -239,50 +283,75 @@
             a = nbuf[l, gb + 2 * rr + r].astype(f32)
             b = ebuf[l, 2 * rr + r].astype(f32)
             for j in range(4):
-                tmp[r, j, 0:48] = a[:, 128 * j : 128 * j + 128]
-                tmp[r, j, 48:56] = b[:, 128 * j : 128 * j + 128]
+                tmp[lr % 2, r, j, 0:48] = a[:, 128 * j : 128 * j + 128]
+                tmp[lr % 2, r, j, 48:56] = b[:, 128 * j : 128 * j + 128]
         for p in range(4):
             for j in range(4):
-                v = tmp[p % 2, j, pl.ds(6 + p // 2, 24, stride=2), :]
+                v = tmp[lr % 2, p % 2, j, pl.ds(6 + p // 2, 24, stride=2), :]
                 col = 512 * p + 128 * j
                 for w in range(2):
                     hx[w, 12 * lr : 12 * lr + 12, col : col + 128] = v[12 * w : 12 * w + 12]
 
-    def merged(w):
-        m = jnp.dot(norm(hx[w], mg[...]), mw[...], preferred_element_type=f32)
-        xc[w] = m.astype(bf16).astype(f32)
-        return xc[w]
+    hold = {}
+
+    def merge(w):
+        def stacked():
+            hold[w] = norm(hx[w], mg[...])
+
+        def product(c):
+            m = jnp.dot(hold[w], mw[:, c : c + 256], preferred_element_type=f32)
+            xc[w, :, c : c + 256] = m.astype(bf16).astype(f32)
+
+        def take():
+            hold[w] = xc[w]
+
+        return [stacked] + [functools.partial(product, c) for c in range(0, 1024, 256)] + [take]
 
     def split(w, y):
-        h = norm((xc[w] + y).astype(bf16).astype(f32), sg[...])
-        hx[w] = jnp.dot(h, sw[...], preferred_element_type=f32)
-
-    attend_windows(2, merged, split, gc[...], wc, wvtc, oc, qkc, vtc, otc, None)
+        def stacked():
+            hold[w] = norm((xc[w] + y).astype(bf16).astype(f32), sg[...])
+
+        def product(c):
+            hx[w, :, c : c + 256] = jnp.dot(hold[w], sw[:, c : c + 256], preferred_element_type=f32)
+
+        def edges():
+            for lr in range(18):
+                l, rr = lr // 6, lr % 6
+                for p in range(4):
+                    for j in range(4):
+                        col = 512 * p + 128 * j
+                        etmp[lr, p % 2, j, pl.ds(p // 2, 3, stride=2), :] = hx[1, 12 * lr + 9 : 12 * lr + 12, col : col + 128]
+                for r in range(2):
+                    sp = jnp.concatenate([etmp[lr, r, j] for j in range(4)], axis=1)
+                    sedge2[l, 2 * rr + r] = (ebuf[l, 2 * rr + r].astype(f32) + sp).astype(bf16)
+            for k in range(4):
+                edge2(k).start()
+
+        steps = [stacked] + [functools.partial(product, c) for c in range(0, 2048, 256)]
+        return steps + [edges] if w == 1 else steps
+
+    attend_windows([1, 0], merge, split, hold, gc[...], wc, wvtc, oc, qc, kc, vtc, otc, None)
     for lr in range(18):
         l, rr = lr // 6, lr % 6
         for p in range(4):
             for j in range(4):
                 col = 512 * p + 128 * j
                 v = jnp.concatenate([hx[w, 12 * lr : 12 * lr + 12, col : col + 128] for w in range(2)], axis=0)
-                tmp[p % 2, j, pl.ds(6 + p // 2, 24, stride=2), :] = v
+                tmp[lr % 2, p % 2, j, pl.ds(6 + p // 2, 24, stride=2), :] = v
         for r in range(2):
-            sp = jnp.concatenate([tmp[r, j] for j in range(4)], axis=1)
+            sp = jnp.concatenate([tmp[lr % 2, r, j] for j in range(4)], axis=1)
             a = nbuf[l, gb + 2 * rr + r].astype(f32)
-            b = ebuf[l, 2 * rr + r].astype(f32)
             jbuf[l, gb + 2 * rr + r] = (a + sp[0:48]).astype(bf16)
-            sedge2[l, 2 * rr + r] = (b + sp[48:56]).astype(bf16)
-    for k in range(4):
-        edge2(k).start()
     rows2.start()
 
     weights[6].wait()
     weights[7].wait()
     wvt[...] = w3[:, 1024:1536].T
 
-    def t3(g):
+    def t3(g, half):
         return remote(
-            comb.at[1 - o, :, pl.ds(9 * g, 3)], comb.at[1 - o, :, pl.ds(6 - 3 * g, 3)], s3.at[g], r3.at[1 - g],
-            dev(2 * g - 1, 0),
+            comb.at[1 - o, half, :, pl.ds(9 * g, 3)], comb.at[1 - o, half, :, pl.ds(6 - 3 * g, 3)],
+            s3.at[2 * g + half], r3.at[2 * (1 - g) + half], dev(2 * g - 1, 0),
         )
 
     def edge3(k):
@@ -314,40 +383,61 @@
 
         def finish(t, y):
             xw[4 * g + t] = xw[4 * g + t] + y
-
-        attend_windows(4, lambda t: xw[4 * g + t], finish, g3[...], w3, wvt, o3, qk_s, vt_s, ot_s, bias.at[g])
-        for lr in range(18):
-            sedge3[lr // 6, 6 * g + lr % 6] = xw[4 * g + 3, 12 * lr + 4 : 12 * lr + 12, :].astype(bf16)
-
-        @pl.when(o == 0)
-        def _():
-            edge3(2 * g).start()
-            edge3(2 * g + 1).start()
-
-        for lr in range(18):
-            slab = jnp.concatenate([xw[4 * g + w, 12 * lr : 12 * lr + 12, :] for w in range(4)], axis=0)
-            comb[1 - o, lr // 6, 6 * g + lr % 6] = slab.astype(bf16)
-        t3(g).start()
+            if t == 3:
+                for lr in range(18):
+                    sedge3[lr // 6, 6 * g + lr % 6] = xw[4 * g + 3, 12 * lr + 4 : 12 * lr + 12, :].astype(bf16)
+
+                @pl.when(o == 0)
+                def _():
+                    edge3(2 * g).start()
+                    edge3(2 * g + 1).start()
+
+            if t % 2 == 1:
+                for lr in range(18):
+                    pair = [xw[4 * g + w, 12 * lr : 12 * lr + 12, :] for w in (t - 1, t)]
+                    comb[1 - o, t // 2, lr // 6, 6 * g + lr % 6] = jnp.concatenate(pair, axis=0).astype(bf16)
+                t3(g, t // 2).start()
+
+        hold = {}
+
+        def begin(t):
+            def take():
+                hold[t] = xw[4 * g + t]
+
+            return [take]
+
+        attend_windows([0, 1, 2, 3], begin, finish, hold, g3[...], w3, wvt, o3, q_s, k_s, vt_s, ot_s, bias.at[g])
         return carry
 
     lax.fori_loop(0, 2, group3, 0)
 
-    for g in (0, 1):
-        remote(
-            comb.at[o, :, pl.ds(0, 3)], comb.at[o, :, pl.ds(3 + 3 * g, 3)], s3.at[g], r3.at[g], dev(1, 0)
-        ).wait_recv()
-        remote(sedge3.at[:, pl.ds(0, 3)], hedge.at[:, pl.ds(3 * g, 3)], s3e.at[g], r3e.at[g], dev(0, 1)).wait_recv()
-    for lr in range(18):
-        l, r = lr // 6, lr % 6
-        e = hedge[l, r].astype(f32)
-        left = comb[0, l, r + 3].astype(f32)
-        right = comb[1, l, r + 3].astype(f32)
-        out_ref[l, r] = jnp.concatenate([e[2:8], left, right[0:42]], axis=0).astype(bf16)
+    def out_copy(b):
+        return pltpu.make_async_copy(final.at[:, pl.ds(3 * b, 3)], out_ref.at[:, pl.ds(3 * b, 3)], osem.at[b])
+
+    def assemble(s, carry):
+        b = o * (1 - s) + (1 - o) * s
+        for half in range(2):
+            remote(
+                comb.at[o, half, :, pl.ds(0, 3)], comb.at[o, half, :, pl.ds(3 + 3 * b, 3)], s3.at[0], r3.at[2 * b + half],
+                dev(1, 0),
+            ).wait_recv()
+        remote(sedge3.at[:, pl.ds(0, 3)], hedge.at[:, pl.ds(3 * b, 3)], s3e.at[0], r3e.at[b], dev(0, 1)).wait_recv()
+        for lr in range(9):
+            l, r = lr // 3, 3 * b + lr % 3
+            halves = [comb[k, half, l, r + 3].astype(f32) for k in range(2) for half in range(2)]
+            parts = [hedge[l, r].astype(f32)[2:8]] + halves[:3] + [halves[3][0:18]]
+            final[l, r] = jnp.concatenate(parts, axis=0).astype(bf16)
+        out_copy(b).start()
+        return carry
+
+    lax.fori_loop(0, 2, assemble, 0)
 
     for g in (0, 1):
         t0a(1 - g).wait_send()
         t0b(1 - g).wait_send()
-        t3(g).wait_send()
+        t3(g, 0).wait_send()
+        t3(g, 1).wait_send()
+        out_copy(g).wait()
     for k in range(4):
         edge1(k).wait_send()
         edge2(k).wait_send()
@@ -371,18 +461,19 @@
     scratch = weights + [
         B(512, 512), B(1024, 1024),
         B(3, 12, 48, 512), B(3, 12, 8, 512), F(8, 216, 512), B(3, 15, 48, 512), B(3, 12, 8, 512), B(3, 12, 8, 512),
-        B(3, 15, 48, 512), B(3, 12, 8, 512), B(3, 12, 8, 512), B(2, 3, 12, 48, 512), B(3, 6, 8, 512), B(3, 12, 8, 512),
-        F(2, 216, 2048), F(2, 216, 1024), F(2, 4, 56, 128), F(2, 216, 216), B(4, 216, 1024), B(4, 512, 216), B(4, 512, 216),
-        B(2, 216, 2048), B(2, 1024, 216), B(2, 1024, 216),
+        B(3, 15, 48, 512), B(3, 12, 8, 512), B(3, 12, 8, 512), B(2, 2, 3, 12, 24, 512), B(3, 6, 8, 512), B(3, 12, 8, 512),
+        F(2, 216, 2048), F(2, 216, 1024), F(2, 2, 4, 56, 128), F(18, 2, 4, 8, 128), F(2, 216, 256),
+        B(4, 256, 512), B(4, 224, 512), B(4, 8, 80, 256), B(4, 512, 216),
+        B(2, 256, 1024), B(2, 224, 1024), B(2, 16, 80, 256), B(2, 1024, 216), B(3, 6, 96, 512),
         D((8,)), D, D, D((2,)), D((2,)), D((2,)), D((2,)), D,
-        D, D, D((4,)), D((4,)), D, D, D((4,)), D((4,)), D((2,)), D((2,)), D((4,)), D((2,)),
+        D, D, D((4,)), D((4,)), D, D, D((4,)), D((4,)), D((4,)), D((4,)), D((4,)), D((2,)), D((2,)),
     ]
     row = lambda g: g.reshape(1, -1)
     return pl.pallas_call(
         mega_kernel,
         out_shape=jax.ShapeDtypeStruct(x.shape, bf16),
         in_specs=[pl.BlockSpec(memory_space=pltpu.SMEM), H, V, H, H, V, H, V, H, H, V, H, V, H, H],
-        out_specs=V,
+        out_specs=H,
         scratch_shapes=scratch,
         compiler_params=pltpu.CompilerParams(
             vmem_limit_bytes=67043328, collective_id=0, has_side_effects=True

time: 67.3 us -> 62.4 us (0.927); the launches traced: 66.2 us -> 62.3 us
  Pallas kernels: 63.4 us -> 59.4 us
    pallas_call x1, Pallas kernels: 63.4 us -> 59.4 us  [mega_call(): pl.pallas_call(mega_kernel, out_shape=jax.ShapeDtypeStruct(x.shape, bf16)...]
where the time goes in v3:
time: 62.4 us; the launch traced here: 62.3 us
  Pallas kernels  59.4 us (95%)
  local copies, waits for them, and re-layouts  2.84 us (5%)
    pallas_call x1, Pallas kernels, mega_call(): pl.pallas_call(mega_kernel, out_shape=jax.ShapeDtypeStruct(x.shape, bf16)...  59.4 us
    unnamed x1, local copies, waits for them, and re-layouts  2.84 us

profile of v3, /device:TPU:1, one launch (start us, length us, event | category | flops | bytes accessed | tf_op | source)
XLA Modules:
  0.0 62.3 jit_solution(14296739163684183690)
XLA Ops:
  0.0 59.4 %section.1 = bf16[3,6,96,512]{3,2,1,0:T(8,128)(2,1)} custom-call(s32[96]{0:T(128)} %lab_ref.1, bf16[3,6,96,512]{3,2,1,0:T(8,128)(2,1)} %x_hbm.1, f32[1,512]{1,0:T(1,128)} %bitcast.8, bf16[512,1536]{1,0:T(8,128)(2,1)} %w1_hbm.1, bf16[512,512]{1,0:T(8,128)(2,1)} %o1_hbm.1, f32[1,2048]{1,0:T(1,128)} %bitcast.5, bf16[2048,1024]{1,0:T(8,128)(2,1)} %mw_hbm.1, ...), custom_call_target="tpu_custom_call" | custom-call | tf_op jit(solution)/shard_map/section/pallas_call | solution.py:472
  59.4 2.8 %copy.17 = bf16[3,6,96,512]{3,2,1,0:T(8,128)(2,1)} copy(bf16[3,6,96,512]{3,2,1,0:T(8,128)(2,1)} %section.1) | data formatting | bytes 3538944

commit v4 on v3

--- a/solution.py
+++ b/solution.py
@@ -76,9 +76,9 @@
             for step in todo[:count]:
                 step()
             todo = todo[count:]
-        for step in later[:2]:
+        for step in later[:4]:
             step()
-        later = later[2:]
+        later = later[4:]
         if k + 3 < len(items):
             ready.append(scores(*items[k + 3]))
         st = ready.pop(0)
@@ -186,9 +186,6 @@
     def _():
         t0c_local().start()
 
-    for copy in weights[2:]:
-        copy.start()
-
     for v in (vt_s, vtc):
         n, heads = v.shape[:2]
         v[:, :, 64:80, :] = jnp.ones((n, heads, 16, 256), bf16)
@@ -223,9 +220,12 @@
         m, far = chunk_to(k)
         return remote(sedge2.at[:, pl.ds(3 * k, 3)], redge.at[:, pl.ds(3 * m, 3)], s2e.at[k], r2e.at[m], dev(far, 1 - o))
 
-    rows1 = remote(
-        nbuf.at[:, pl.ds(12 * (1 - o), 3)], nbuf.at[:, pl.ds(12 * o, 3)], s1, r1, dev(2 - 4 * o, 0)
-    )
+    rows1 = [
+        remote(
+            nbuf.at[k, :, pl.ds(12 * (1 - o), 3)], nbuf.at[k, :, pl.ds(12 * o, 3)], s1.at[k], r1.at[k], dev(2 - 4 * o, 0)
+        )
+        for k in range(2)
+    ]
     rows2 = remote(
         jbuf.at[:, pl.ds(12 * o, 3)], jbuf.at[:, pl.ds(12 * (1 - o), 3)], s2, r2, dev(4 * o - 2, 0)
     )
@@ -234,6 +234,12 @@
         g = (1 - o) * (1 - s) + o * s
         t0a(1 - g).wait_recv()
         t0b(1 - g).wait_recv()
+
+        @pl.when(s == 0)
+        def _():
+            for copy in weights[2:]:
+                copy.start()
+
         for lr in range(18):
             a = xa[lr // 6, 6 * g + lr % 6].astype(f32)
             b = xb[lr // 6, 6 * g + lr % 6].astype(f32)
@@ -249,6 +255,14 @@
                     sedge[lr // 6, 6 * g + lr % 6] = xw[4 * g, 12 * lr : 12 * lr + 8, :].astype(bf16)
                 edge1(2 * g).start()
                 edge1(2 * g + 1).start()
+            if t % 2 == 1:
+                for lr in range(18):
+                    pair = [xw[4 * g + w, 12 * lr : 12 * lr + 12, :] for w in (t - 1, t)]
+                    nbuf[t // 2, lr // 6, fb + 6 * g + lr % 6] = jnp.concatenate(pair, axis=0).astype(bf16)
+
+                @pl.when(s == 0)
+                def _():
+                    rows1[t // 2].start()
 
         hold = {}
 
@@ -259,14 +273,6 @@
             return [take]
 
         attend_windows([0, 1, 2, 3], begin, finish, hold, g1[...], w1, wvt, o1, q_s, k_s, vt_s, ot_s, bias.at[g])
-        for lr in range(18):
-            slab = jnp.concatenate([xw[4 * g + w, 12 * lr : 12 * lr + 12, :] for w in range(4)], axis=0)
-            nbuf[lr // 6, fb + 6 * g + lr % 6] = slab.astype(bf16)
-
-        @pl.when(s == 0)
-        def _():
-            rows1.start()
-
         return carry
 
     lax.fori_loop(0, 2, group1, 0)
@@ -274,16 +280,18 @@
     for copy in weights[2:6]:
         copy.wait()
     wvtc[...] = wc[:, 2048:3072].T
-    rows1.wait_recv()
+    for k in range(2):
+        rows1[k].wait_recv()
     for k in range(4):
         edge1(k).wait_recv()
     for lr in range(18):
         l, rr = lr // 6, lr % 6
         for r in range(2):
-            a = nbuf[l, gb + 2 * rr + r].astype(f32)
+            a = [nbuf[k, l, gb + 2 * rr + r].astype(f32) for k in range(2)]
             b = ebuf[l, 2 * rr + r].astype(f32)
             for j in range(4):
-                tmp[lr % 2, r, j, 0:48] = a[:, 128 * j : 128 * j + 128]
+                for k in range(2):
+                    tmp[lr % 2, r, j, 24 * k : 24 * k + 24] = a[k][:, 128 * j : 128 * j + 128]
                 tmp[lr % 2, r, j, 48:56] = b[:, 128 * j : 128 * j + 128]
         for p in range(4):
             for j in range(4):
@@ -340,7 +348,7 @@
                 tmp[lr % 2, p % 2, j, pl.ds(6 + p // 2, 24, stride=2), :] = v
         for r in range(2):
             sp = jnp.concatenate([tmp[lr % 2, r, j] for j in range(4)], axis=1)
-            a = nbuf[l, gb + 2 * rr + r].astype(f32)
+            a = jnp.concatenate([nbuf[k, l, gb + 2 * rr + r].astype(f32) for k in range(2)], axis=0)
             jbuf[l, gb + 2 * rr + r] = (a + sp[0:48]).astype(bf16)
     rows2.start()
 
@@ -362,22 +370,12 @@
     def group3(s, carry):
         g = o * (1 - s) + (1 - o) * s
 
-        def landed(k, carry):
-            m = 2 * g + k
-            remote(sedge2.at[:, pl.ds(0, 3)], redge.at[:, pl.ds(3 * m, 3)], s2e.at[0], r2e.at[m], dev(1, 0)).wait_recv()
-            return carry
-
-        lax.fori_loop(0, 2, landed, 0)
-
         @pl.when(s == 1)
         def _():
             rows2.wait_recv()
 
         for lr in range(18):
             a = jbuf[lr // 6, fb + 6 * g + lr % 6].astype(f32)
-            b = redge[lr // 6, 6 * g + lr % 6].astype(f32)
-            xw[4 * g, 12 * lr : 12 * lr + 6, :] = b[0:6]
-            xw[4 * g, 12 * lr + 6 : 12 * lr + 12, :] = a[6:12]
             for w in range(1, 4):
                 xw[4 * g + w, 12 * lr : 12 * lr + 12, :] = a[12 * w : 12 * w + 12]
 
@@ -392,21 +390,30 @@
                     edge3(2 * g).start()
                     edge3(2 * g + 1).start()
 
-            if t % 2 == 1:
+            if t % 2 == 0:
                 for lr in range(18):
-                    pair = [xw[4 * g + w, 12 * lr : 12 * lr + 12, :] for w in (t - 1, t)]
+                    pair = [xw[4 * g + w, 12 * lr : 12 * lr + 12, :] for w in (t, t + 1)]
                     comb[1 - o, t // 2, lr // 6, 6 * g + lr % 6] = jnp.concatenate(pair, axis=0).astype(bf16)
                 t3(g, t // 2).start()
 
         hold = {}
 
         def begin(t):
+            def landed():
+                for m in range(2):
+                    remote(
+                        sedge2.at[:, pl.ds(0, 3)], redge.at[:, pl.ds(6 * g + 3 * m, 3)], s2e.at[0], r2e.at[2 * g + m], dev(1, 0)
+                    ).wait_recv()
+                for lr in range(18):
+                    xw[4 * g, 12 * lr : 12 * lr + 6, :] = redge[lr // 6, 6 * g + lr % 6].astype(f32)[0:6]
+                    xw[4 * g, 12 * lr + 6 : 12 * lr + 12, :] = jbuf[lr // 6, fb + 6 * g + lr % 6].astype(f32)[6:12]
+
             def take():
                 hold[t] = xw[4 * g + t]
 
-            return [take]
-
-        attend_windows([0, 1, 2, 3], begin, finish, hold, g3[...], w3, wvt, o3, q_s, k_s, vt_s, ot_s, bias.at[g])
+            return [landed, take] if t == 0 else [take]
+
+        attend_windows([3, 2, 1, 0], begin, finish, hold, g3[...], w3, wvt, o3, q_s, k_s, vt_s, ot_s, bias.at[g])
         return carry
 
     lax.fori_loop(0, 2, group3, 0)
@@ -441,7 +448,8 @@
     for k in range(4):
         edge1(k).wait_send()
         edge2(k).wait_send()
-    rows1.wait_send()
+    for k in range(2):
+        rows1[k].wait_send()
     rows2.wait_send()
 
     @pl.when(o == 0)
@@ -460,13 +468,13 @@
     weights = [B(*a.shape) for a in (w1, o1, mw, wc, oc, sw, w3, o3)]
     scratch = weights + [
         B(512, 512), B(1024, 1024),
-        B(3, 12, 48, 512), B(3, 12, 8, 512), F(8, 216, 512), B(3, 15, 48, 512), B(3, 12, 8, 512), B(3, 12, 8, 512),
+        B(3, 12, 48, 512), B(3, 12, 8, 512), F(8, 216, 512), B(2, 3, 15, 24, 512), B(3, 12, 8, 512), B(3, 12, 8, 512),
         B(3, 15, 48, 512), B(3, 12, 8, 512), B(3, 12, 8, 512), B(2, 2, 3, 12, 24, 512), B(3, 6, 8, 512), B(3, 12, 8, 512),
         F(2, 216, 2048), F(2, 216, 1024), F(2, 2, 4, 56, 128), F(18, 2, 4, 8, 128), F(2, 216, 256),
         B(4, 256, 512), B(4, 224, 512), B(4, 8, 80, 256), B(4, 512, 216),
         B(2, 256, 1024), B(2, 224, 1024), B(2, 16, 80, 256), B(2, 1024, 216), B(3, 6, 96, 512),
         D((8,)), D, D, D((2,)), D((2,)), D((2,)), D((2,)), D,
-        D, D, D((4,)), D((4,)), D, D, D((4,)), D((4,)), D((4,)), D((4,)), D((4,)), D((2,)), D((2,)),
+        D((2,)), D((2,)), D((4,)), D((4,)), D, D, D((4,)), D((4,)), D((4,)), D((4,)), D((4,)), D((2,)), D((2,)),
     ]
     row = lambda g: g.reshape(1, -1)
     return pl.pallas_call(

time: 62.4 us -> 58.5 us (0.938)
  Pallas kernels: 59.4 us -> 55.4 us
    pallas_call x1, Pallas kernels: 59.4 us -> 55.4 us  [mega_call(): pl.pallas_call(mega_kernel, out_shape=jax.ShapeDtypeStruct(x.shape, bf16)...]
where the time goes in v4:
time: 58.5 us; the launch traced here: 58.3 us
  Pallas kernels  55.4 us (95%)
  local copies, waits for them, and re-layouts  2.84 us (5%)
    pallas_call x1, Pallas kernels, mega_call(): pl.pallas_call(mega_kernel, out_shape=jax.ShapeDtypeStruct(x.shape, bf16)...  55.4 us
    unnamed x1, local copies, waits for them, and re-layouts  2.84 us

profile of v4, /device:TPU:1, one launch (start us, length us, event | category | flops | bytes accessed | tf_op | source)
XLA Modules:
  0.0 58.3 jit_solution(9695033145609585539)
XLA Ops:
  0.0 55.4 %section.1 = bf16[3,6,96,512]{3,2,1,0:T(8,128)(2,1)} custom-call(s32[96]{0:T(128)} %lab_ref.1, bf16[3,6,96,512]{3,2,1,0:T(8,128)(2,1)} %x_hbm.1, f32[1,512]{1,0:T(1,128)} %bitcast.8, bf16[512,1536]{1,0:T(8,128)(2,1)} %w1_hbm.1, bf16[512,512]{1,0:T(8,128)(2,1)} %o1_hbm.1, f32[1,2048]{1,0:T(1,128)} %bitcast.5, bf16[2048,1024]{1,0:T(8,128)(2,1)} %mw_hbm.1, ...), custom_call_target="tpu_custom_call" | custom-call | tf_op jit(solution)/shard_map/section/pallas_call | solution.py:480
  55.5 2.8 %copy.17 = bf16[3,6,96,512]{3,2,1,0:T(8,128)(2,1)} copy(bf16[3,6,96,512]{3,2,1,0:T(8,128)(2,1)} %section.1) | data formatting | bytes 3538944

commit v5 on v4

--- a/solution.py
+++ b/solution.py
@@ -226,9 +226,12 @@
         )
         for k in range(2)
     ]
-    rows2 = remote(
-        jbuf.at[:, pl.ds(12 * o, 3)], jbuf.at[:, pl.ds(12 * (1 - o), 3)], s2, r2, dev(4 * o - 2, 0)
-    )
+    rows2 = [
+        remote(
+            jbuf.at[k, :, pl.ds(12 * o, 3)], jbuf.at[k, :, pl.ds(12 * (1 - o), 3)], s2.at[k], r2.at[k], dev(4 * o - 2, 0)
+        )
+        for k in range(2)
+    ]
 
     def group1(s, carry):
         g = (1 - o) * (1 - s) + o * s
@@ -348,9 +351,11 @@
                 tmp[lr % 2, p % 2, j, pl.ds(6 + p // 2, 24, stride=2), :] = v
         for r in range(2):
             sp = jnp.concatenate([tmp[lr % 2, r, j] for j in range(4)], axis=1)
-            a = jnp.concatenate([nbuf[k, l, gb + 2 * rr + r].astype(f32) for k in range(2)], axis=0)
-            jbuf[l, gb + 2 * rr + r] = (a + sp[0:48]).astype(bf16)
-    rows2.start()
+            for k in range(2):
+                a = nbuf[k, l, gb + 2 * rr + r].astype(f32)
+                jbuf[k, l, gb + 2 * rr + r] = (a + sp[24 * k : 24 * k + 24]).astype(bf16)
+    rows2[1].start()
+    rows2[0].start()
 
     weights[6].wait()
     weights[7].wait()
@@ -372,12 +377,12 @@
 
         @pl.when(s == 1)
         def _():
-            rows2.wait_recv()
+            rows2[1].wait_recv()
 
         for lr in range(18):
-            a = jbuf[lr // 6, fb + 6 * g + lr % 6].astype(f32)
-            for w in range(1, 4):
-                xw[4 * g + w, 12 * lr : 12 * lr + 12, :] = a[12 * w : 12 * w + 12]
+            a = jbuf[1, lr // 6, fb + 6 * g + lr % 6].astype(f32)
+            for w in range(2):
+                xw[4 * g + 2 + w, 12 * lr : 12 * lr + 12, :] = a[12 * w : 12 * w + 12]
 
         def finish(t, y):
             xw[4 * g + t] = xw[4 * g + t] + y
@@ -399,6 +404,15 @@
         hold = {}
 
         def begin(t):
+            def half():
+                @pl.when(s == 1)
+                def _():
+                    rows2[0].wait_recv()
+
+                for lr in range(18):
+                    a = jbuf[0, lr // 6, fb + 6 * g + lr % 6].astype(f32)
+                    xw[4 * g + 1, 12 * lr : 12 * lr + 12, :] = a[12:24]
+
             def landed():
                 for m in range(2):
                     remote(
@@ -406,12 +420,12 @@
                     ).wait_recv()
                 for lr in range(18):
                     xw[4 * g, 12 * lr : 12 * lr + 6, :] = redge[lr // 6, 6 * g + lr % 6].astype(f32)[0:6]
-                    xw[4 * g, 12 * lr + 6 : 12 * lr + 12, :] = jbuf[lr // 6, fb + 6 * g + lr % 6].astype(f32)[6:12]
+                    xw[4 * g, 12 * lr + 6 : 12 * lr + 12, :] = jbuf[0, lr // 6, fb + 6 * g + lr % 6].astype(f32)[6:12]
 
             def take():
                 hold[t] = xw[4 * g + t]
 
-            return [landed, take] if t == 0 else [take]
+            return {0: [landed], 1: [half]}.get(t, []) + [take]
 
         attend_windows([3, 2, 1, 0], begin, finish, hold, g3[...], w3, wvt, o3, q_s, k_s, vt_s, ot_s, bias.at[g])
         return carry
@@ -450,7 +464,8 @@
         edge2(k).wait_send()
     for k in range(2):
         rows1[k].wait_send()
-    rows2.wait_send()
+    for k in range(2):
+        rows2[k].wait_send()
 
     @pl.when(o == 0)
     def _():
@@ -469,12 +484,12 @@
     scratch = weights + [
         B(512, 512), B(1024, 1024),
         B(3, 12, 48, 512), B(3, 12, 8, 512), F(8, 216, 512), B(2, 3, 15, 24, 512), B(3, 12, 8, 512), B(3, 12, 8, 512),
-        B(3, 15, 48, 512), B(3, 12, 8, 512), B(3, 12, 8, 512), B(2, 2, 3, 12, 24, 512), B(3, 6, 8, 512), B(3, 12, 8, 512),
+        B(2, 3, 15, 24, 512), B(3, 12, 8, 512), B(3, 12, 8, 512), B(2, 2, 3, 12, 24, 512), B(3, 6, 8, 512), B(3, 12, 8, 512),
         F(2, 216, 2048), F(2, 216, 1024), F(2, 2, 4, 56, 128), F(18, 2, 4, 8, 128), F(2, 216, 256),
         B(4, 256, 512), B(4, 224, 512), B(4, 8, 80, 256), B(4, 512, 216),
         B(2, 256, 1024), B(2, 224, 1024), B(2, 16, 80, 256), B(2, 1024, 216), B(3, 6, 96, 512),
         D((8,)), D, D, D((2,)), D((2,)), D((2,)), D((2,)), D,
-        D((2,)), D((2,)), D((4,)), D((4,)), D, D, D((4,)), D((4,)), D((4,)), D((4,)), D((4,)), D((2,)), D((2,)),
+        D((2,)), D((2,)), D((4,)), D((4,)), D((2,)), D((2,)), D((4,)), D((4,)), D((4,)), D((4,)), D((4,)), D((2,)), D((2,)),
     ]
     row = lambda g: g.reshape(1, -1)
     return pl.pallas_call(

time: 58.5 us -> 58.9 us (level)
  no operation moved by 1% of the time
where the time goes in v5:
time: 58.9 us; the launch traced here: 58.7 us
  Pallas kernels  55.9 us (95%)
  local copies, waits for them, and re-layouts  2.84 us (5%)
    pallas_call x1, Pallas kernels, mega_call(): pl.pallas_call(mega_kernel, out_shape=jax.ShapeDtypeStruct(x.shape, bf16)...  55.9 us
    unnamed x1, local copies, waits for them, and re-layouts  2.84 us

profile of v5, /device:TPU:1, one launch (start us, length us, event | category | flops | bytes accessed | tf_op | source)
XLA Modules:
  0.0 58.7 jit_solution(7515148489669207233)
XLA Ops:
  0.0 55.9 %section.1 = bf16[3,6,96,512]{3,2,1,0:T(8,128)(2,1)} custom-call(s32[96]{0:T(128)} %lab_ref.1, bf16[3,6,96,512]{3,2,1,0:T(8,128)(2,1)} %x_hbm.1, f32[1,512]{1,0:T(1,128)} %bitcast.8, bf16[512,1536]{1,0:T(8,128)(2,1)} %w1_hbm.1, bf16[512,512]{1,0:T(8,128)(2,1)} %o1_hbm.1, f32[1,2048]{1,0:T(1,128)} %bitcast.5, bf16[2048,1024]{1,0:T(8,128)(2,1)} %mw_hbm.1, ...), custom_call_target="tpu_custom_call" | custom-call | tf_op jit(solution)/shard_map/section/pallas_call | solution.py:495
  55.9 2.8 %copy.17 = bf16[3,6,96,512]{3,2,1,0:T(8,128)(2,1)} copy(bf16[3,6,96,512]{3,2,1,0:T(8,128)(2,1)} %section.1) | data formatting | bytes 3538944
